TPU v7x, 32 devices: a whole 2x2x4 slice. The times are simulated.
32 devices in a mesh: dev: 8 (over y, x, core), rep: 4 (over z).
Axes of the slice: x: 2, y: 2, z: 4, core: 2. Of those that a mesh axis runs over, the one named last changes fastest.
Arguments:
- images: bfloat16 [64, 577, 1024], P(('dev', 'rep')), may hold values from -6 to 6
- norm1_gain: bfloat16 [1024], P(('dev', 'rep')), may hold values from 0.25 to 1.75
- norm1_bias: bfloat16 [1024], P(('dev', 'rep')), may hold values from -3 to 3
- qkv_weight: bfloat16 [1024, 3072], P(('dev', 'rep')), may hold values from -0.1875 to 0.1875
- qv_bias: bfloat16 [2048], P(('dev', 'rep')), may hold values from -1.1953125 to 1.1953125
- out_weight: bfloat16 [1024, 1024], P(('dev', 'rep')), may hold values from -0.75 to 0.75
- out_bias: bfloat16 [1024], P(('dev', 'rep')), may hold values from -3 to 3
- norm2_gain: bfloat16 [1024], P(('dev', 'rep')), may hold values from 0.25 to 1.75
- norm2_bias: bfloat16 [1024], P(('dev', 'rep')), may hold values from -3 to 3
- up_weight: bfloat16 [1024, 4096], P(('dev', 'rep')), may hold values from -0.1875 to 0.1875
- up_bias: bfloat16 [4096], P(('dev', 'rep')), may hold values from -3 to 3
- down_weight: bfloat16 [4096, 1024], P(('dev', 'rep')), may hold values from -0.125 to 0.125
- down_bias: bfloat16 [1024], P(('dev', 'rep')), may hold values from -3 to 3
- cotangent: bfloat16 [64, 577, 1024], P(('dev', 'rep')), may hold values from -6 to 6
- filled: int32 [64], P(('dev', 'rep')), may hold values 0 or 1
Outputs:
- output: bfloat16 [64, 577, 1024], P(('dev', 'rep'))
- input_grad: bfloat16 [64, 577, 1024], P(('dev', 'rep'))
- norm1_gain_grad: float32 [1024], P(('dev', 'rep'))
- norm1_bias_grad: float32 [1024], P(('dev', 'rep'))
- qkv_weight_grad: float32 [1024, 3072], P(('dev', 'rep'))
- qv_bias_grad: float32 [2048], P(('dev', 'rep'))
- out_weight_grad: float32 [1024, 1024], P(('dev', 'rep'))
- out_bias_grad: float32 [1024], P(('dev', 'rep'))
- norm2_gain_grad: float32 [1024], P(('dev', 'rep'))
- norm2_bias_grad: float32 [1024], P(('dev', 'rep'))
- up_weight_grad: float32 [1024, 4096], P(('dev', 'rep'))
- up_bias_grad: float32 [4096], P(('dev', 'rep'))
- down_weight_grad: float32 [4096, 1024], P(('dev', 'rep'))
- down_bias_grad: float32 [1024], P(('dev', 'rep'))
Inputs may be any that keep to these rules, and one draw needn't show every extreme that they name: `filled`: 1 marks a slot that holds an image, 0 an empty slot.
All inputs are finite; a program needn't handle non-finite values. No bound on the sum of `filled` on one device may be relied on, other than what follows from the above.
Results may differ from a plain program's by a relative error of at most 0.012.
Values may be sent and summed in bfloat16 or wider, within the bound.
A program may use at most 320 MiB of HBM per device.

v0:
```python
import math

import jax
import jax.numpy as jnp
from jax import lax
from jax.sharding import PartitionSpec as P

HEADS = 16
HD = 64
MICRO = 2


def layer_norm(values, gain, shift):
    centred = values - jnp.mean(values, axis=-1, keepdims=True)
    spread = jnp.mean(centred * centred, axis=-1, keepdims=True)
    return centred * lax.rsqrt(spread + 1e-06) * gain + shift


def gelu_exact(values):
    return jax.nn.gelu(values, approximate=False)


def inner_rows(left, right):
    return lax.dot_general(
        left, right, (((0,), (0,)), ((), ())), preferred_element_type=jnp.float32
    )


def times_trans(left, right):
    return lax.dot_general(
        left, right, (((1,), (1,)), ((), ())), preferred_element_type=jnp.float32
    )


def attend(queries, keys, values, scale):
    scores = jnp.einsum("qhd,khd->hqk", queries, keys, preferred_element_type=jnp.float32) * scale
    highest = jnp.max(scores, axis=-1, keepdims=True)
    raised = jnp.exp(scores - highest)
    totals = jnp.sum(raised, axis=-1, keepdims=True)
    probs = (raised / totals).astype(jnp.bfloat16)
    mixed = jnp.einsum("hqk,khd->qhd", probs, values, preferred_element_type=jnp.float32)
    return (mixed, highest + jnp.log(totals))


def attend_back(queries, keys, values, heads_grad, log_totals, scale):
    scores = jnp.einsum("qhd,khd->hqk", queries, keys, preferred_element_type=jnp.float32) * scale
    probs = jnp.exp(scores - log_totals)
    probs_low = probs.astype(jnp.bfloat16)
    value_grad = jnp.einsum(
        "hqk,qhd->khd", probs_low, heads_grad, preferred_element_type=jnp.float32
    )
    prob_grad = jnp.einsum("qhd,khd->hqk", heads_grad, values, preferred_element_type=jnp.float32)
    score_grad = probs * (prob_grad - jnp.sum(probs * prob_grad, axis=-1, keepdims=True))
    score_low = score_grad.astype(jnp.bfloat16)
    query_grad = (
        jnp.einsum("hqk,khd->qhd", score_low, keys, preferred_element_type=jnp.float32) * scale
    )
    key_grad = (
        jnp.einsum("hqk,qhd->khd", score_low, queries, preferred_element_type=jnp.float32) * scale
    )
    return (query_grad, key_grad, value_grad)


def run_forward(block, gathered, scale):
    (
        gain_one,
        bias_one,
        joint_weight,
        joint_bias,
        proj_weight,
        proj_bias,
        gain_two,
        bias_two,
        up_mat,
        up_vec,
        down_mat,
        down_vec,
    ) = gathered
    images_now, seq_len, width = block.shape
    row_count = images_now * seq_len
    residual_in = block.astype(jnp.float32).reshape(row_count, width)
    normed_one = layer_norm(
        residual_in, gain_one.astype(jnp.float32), bias_one.astype(jnp.float32)
    ).astype(jnp.bfloat16)
    joint_float = joint_bias.astype(jnp.float32)
    bias_full = jnp.concatenate(
        [joint_float[:width], jnp.zeros((width,), jnp.float32), joint_float[width:]]
    )
    joined = (
        jnp.dot(normed_one, joint_weight, preferred_element_type=jnp.float32) + bias_full
    ).astype(jnp.bfloat16)
    parts = joined.reshape(images_now, seq_len, 3, HEADS, HD)
    queries = parts[:, :, 0]
    keys = parts[:, :, 1]
    values = parts[:, :, 2]
    mixed, log_totals = lax.map(
        lambda item: attend(item[0], item[1], item[2], scale), (queries, keys, values)
    )
    heads_low = mixed.reshape(row_count, width).astype(jnp.bfloat16)
    middle = (
        residual_in
        + jnp.dot(heads_low, proj_weight, preferred_element_type=jnp.float32)
        + proj_bias.astype(jnp.float32)
    )
    normed_two = layer_norm(
        middle, gain_two.astype(jnp.float32), bias_two.astype(jnp.float32)
    ).astype(jnp.bfloat16)
    hidden_pre = jnp.dot(normed_two, up_mat, preferred_element_type=jnp.float32) + up_vec.astype(
        jnp.float32
    )
    activated = gelu_exact(hidden_pre).astype(jnp.bfloat16)
    result = (
        middle
        + jnp.dot(activated, down_mat, preferred_element_type=jnp.float32)
        + down_vec.astype(jnp.float32)
    )
    kept = (
        residual_in,
        normed_one,
        queries,
        keys,
        values,
        log_totals,
        heads_low,
        middle,
        normed_two,
        hidden_pre,
        activated,
    )
    return (kept, result.astype(jnp.bfloat16).reshape(block.shape))


def run_backward(kept, gathered, grad_in, scale):
    (
        gain_one,
        bias_one,
        joint_weight,
        joint_bias,
        proj_weight,
        proj_bias,
        gain_two,
        bias_two,
        up_mat,
        up_vec,
        down_mat,
        down_vec,
    ) = gathered
    (
        residual_in,
        normed_one,
        queries,
        keys,
        values,
        log_totals,
        heads_low,
        middle,
        normed_two,
        hidden_pre,
        activated,
    ) = kept
    row_count, width = residual_in.shape
    branch_grad = grad_in.astype(jnp.bfloat16)
    down_vec_grad = jnp.sum(branch_grad, axis=0, dtype=jnp.float32)
    down_mat_grad = inner_rows(activated, branch_grad)
    act_grad = times_trans(branch_grad, down_mat)
    gelu_pull = jax.vjp(gelu_exact, hidden_pre)[1]
    pre_grad = gelu_pull(act_grad)[0].astype(jnp.bfloat16)
    up_vec_grad = jnp.sum(pre_grad, axis=0, dtype=jnp.float32)
    up_mat_grad = inner_rows(normed_two, pre_grad)
    norm_two_in = times_trans(pre_grad, up_mat)
    pull_two = jax.vjp(
        layer_norm, middle, gain_two.astype(jnp.float32), bias_two.astype(jnp.float32)
    )[1]
    middle_part, gain_two_grad, bias_two_grad = pull_two(norm_two_in)
    middle_grad = grad_in + middle_part
    attn_grad = middle_grad.astype(jnp.bfloat16)
    proj_bias_grad = jnp.sum(attn_grad, axis=0, dtype=jnp.float32)
    proj_weight_grad = inner_rows(heads_low, attn_grad)
    heads_grad = times_trans(attn_grad, proj_weight).astype(jnp.bfloat16).reshape(queries.shape)
    query_grad, key_grad, value_grad = lax.map(
        lambda item: attend_back(item[0], item[1], item[2], item[3], item[4], scale),
        (queries, keys, values, heads_grad, log_totals),
    )
    joined_grad = (
        jnp.stack([query_grad, key_grad, value_grad], axis=2)
        .astype(jnp.bfloat16)
        .reshape(row_count, 3 * width)
    )
    column_sums = jnp.sum(joined_grad, axis=0, dtype=jnp.float32)
    joint_bias_grad = jnp.concatenate([column_sums[:width], column_sums[2 * width :]])
    joint_weight_grad = inner_rows(normed_one, joined_grad)
    norm_one_in = times_trans(joined_grad, joint_weight)
    pull_one = jax.vjp(
        layer_norm, residual_in, gain_one.astype(jnp.float32), bias_one.astype(jnp.float32)
    )[1]
    input_part, gain_one_grad, bias_one_grad = pull_one(norm_one_in)
    image_grad = middle_grad + input_part
    grads = (
        gain_one_grad,
        bias_one_grad,
        joint_weight_grad,
        joint_bias_grad,
        proj_weight_grad,
        proj_bias_grad,
        gain_two_grad,
        bias_two_grad,
        up_mat_grad,
        up_vec_grad,
        down_mat_grad,
        down_vec_grad,
    )
    return (grads, image_grad)


def fetch_forward(shards):
    return (
        lax.all_gather(shards[0], ("dev", "rep"), axis=0, tiled=True),
        lax.all_gather(shards[1], ("dev", "rep"), axis=0, tiled=True),
        lax.all_gather(shards[2], ("dev", "rep"), axis=0, tiled=True),
        lax.all_gather(shards[3], ("dev", "rep"), axis=0, tiled=True),
        lax.all_gather(shards[4], ("dev", "rep"), axis=0, tiled=True),
        lax.all_gather(shards[5], ("dev", "rep"), axis=0, tiled=True),
        lax.all_gather(shards[6], ("dev", "rep"), axis=0, tiled=True),
        lax.all_gather(shards[7], ("dev", "rep"), axis=0, tiled=True),
        lax.all_gather(shards[8], ("dev", "rep"), axis=0, tiled=True),
        lax.all_gather(shards[9], ("dev", "rep"), axis=0, tiled=True),
        lax.all_gather(shards[10], ("dev", "rep"), axis=0, tiled=True),
        lax.all_gather(shards[11], ("dev", "rep"), axis=0, tiled=True),
    )


def body(
    images,
    norm1_gain,
    norm1_bias,
    qkv_weight,
    qv_bias,
    out_weight,
    out_bias,
    norm2_gain,
    norm2_bias,
    up_weight,
    up_bias,
    down_weight,
    down_bias,
    cotangent,
    filled,
):
    per_step = images.shape[0] // MICRO
    seq_len = images.shape[1]
    width = images.shape[2]
    row_count = per_step * seq_len
    scale = 1.0 / math.sqrt(HD)
    shards = (
        norm1_gain,
        norm1_bias,
        qkv_weight,
        qv_bias,
        out_weight,
        out_bias,
        norm2_gain,
        norm2_bias,
        up_weight,
        up_bias,
        down_weight,
        down_bias,
    )
    outputs = []
    image_grads = []
    shares = None
    for micro_step in range(MICRO):
        first_image = micro_step * per_step
        block = images[first_image : first_image + per_step]
        gathered = fetch_forward(shards)
        kept, result = run_forward(block, gathered, scale)
        outputs.append(result)
        backward_weights = (
            lax.all_gather(norm1_gain, ("dev", "rep"), axis=0, tiled=True),
            lax.all_gather(norm1_bias, ("dev", "rep"), axis=0, tiled=True),
            lax.all_gather(qkv_weight, ("dev", "rep"), axis=0, tiled=True),
            lax.all_gather(qv_bias, ("dev", "rep"), axis=0, tiled=True),
            lax.all_gather(out_weight, ("dev", "rep"), axis=0, tiled=True),
            lax.all_gather(out_bias, ("dev", "rep"), axis=0, tiled=True),
            lax.all_gather(norm2_gain, ("dev", "rep"), axis=0, tiled=True),
            lax.all_gather(norm2_bias, ("dev", "rep"), axis=0, tiled=True),
            lax.all_gather(up_weight, ("dev", "rep"), axis=0, tiled=True),
            lax.all_gather(up_bias, ("dev", "rep"), axis=0, tiled=True),
            lax.all_gather(down_weight, ("dev", "rep"), axis=0, tiled=True),
            lax.all_gather(down_bias, ("dev", "rep"), axis=0, tiled=True),
        )
        flags = filled[first_image : first_image + per_step].astype(jnp.float32)
        grad_in = (
            cotangent[first_image : first_image + per_step].astype(jnp.float32)
            * flags[:, None, None]
        ).reshape(row_count, width)
        grads, image_grad = run_backward(kept, backward_weights, grad_in, scale)
        image_grads.append(image_grad.astype(jnp.bfloat16).reshape(block.shape))
        part_sums = (
            lax.psum_scatter(grads[0], ("dev", "rep"), scatter_dimension=0, tiled=True),
            lax.psum_scatter(grads[1], ("dev", "rep"), scatter_dimension=0, tiled=True),
            lax.psum_scatter(grads[2], ("dev", "rep"), scatter_dimension=0, tiled=True),
            lax.psum_scatter(grads[3], ("dev", "rep"), scatter_dimension=0, tiled=True),
            lax.psum_scatter(grads[4], ("dev", "rep"), scatter_dimension=0, tiled=True),
            lax.psum_scatter(grads[5], ("dev", "rep"), scatter_dimension=0, tiled=True),
            lax.psum_scatter(grads[6], ("dev", "rep"), scatter_dimension=0, tiled=True),
            lax.psum_scatter(grads[7], ("dev", "rep"), scatter_dimension=0, tiled=True),
            lax.psum_scatter(grads[8], ("dev", "rep"), scatter_dimension=0, tiled=True),
            lax.psum_scatter(grads[9], ("dev", "rep"), scatter_dimension=0, tiled=True),
            lax.psum_scatter(grads[10], ("dev", "rep"), scatter_dimension=0, tiled=True),
            lax.psum_scatter(grads[11], ("dev", "rep"), scatter_dimension=0, tiled=True),
        )
        shares = part_sums if shares is None else jax.tree.map(jnp.add, shares, part_sums)
    output = jnp.concatenate(outputs, axis=0)
    input_grad = jnp.concatenate(image_grads, axis=0)
    return (
        output,
        input_grad,
        shares[0],
        shares[1],
        shares[2],
        shares[3],
        shares[4],
        shares[5],
        shares[6],
        shares[7],
        shares[8],
        shares[9],
        shares[10],
        shares[11],
    )


def solution(mesh):
    in_specs = (
        P(("dev", "rep"), None, None),
        P(("dev", "rep")),
        P(("dev", "rep")),
        P(("dev", "rep"), None),
        P(("dev", "rep")),
        P(("dev", "rep"), None),
        P(("dev", "rep")),
        P(("dev", "rep")),
        P(("dev", "rep")),
        P(("dev", "rep"), None),
        P(("dev", "rep")),
        P(("dev", "rep"), None),
        P(("dev", "rep")),
        P(("dev", "rep"), None, None),
        P(("dev", "rep")),
    )
    out_specs = (
        P(("dev", "rep"), None, None),
        P(("dev", "rep"), None, None),
        P(("dev", "rep")),
        P(("dev", "rep")),
        P(("dev", "rep"), None),
        P(("dev", "rep")),
        P(("dev", "rep"), None),
        P(("dev", "rep")),
        P(("dev", "rep")),
        P(("dev", "rep")),
        P(("dev", "rep"), None),
        P(("dev", "rep")),
        P(("dev", "rep"), None),
        P(("dev", "rep")),
    )
    return jax.shard_map(body, mesh=mesh, in_specs=in_specs, out_specs=out_specs, check_vma=False)
```

profile of v0, /device:TPU:0, one launch (start us, length us, event | category | flops | bytes accessed | tf_op | source)
XLA Modules:
  0.0 1488.6 jit_solution(12618038280445305222)
XLA Ops:
  18.5 42.6 %all-reduce.16 = (bf16[2048]{0:T(1024)(128)(2,1)S(1)}, bf16[1024]{0:T(1024)(128)(2,1)S(1)}, bf16[1024]{0:T(1024)(128)(2,1)S(1)}, bf16[1024]{0:T(1024)(128)(2,1)S...) all-reduce(bf16[2048]{0:T(1024)(128)(2,1)S(1)} %dynamic-update-slic, ...), channel_id=1, replica_groups=mesh['dev'=8,'rep'=4] {'dev','rep'}, use_global_device_ids=true, to_apply=%add.2 | all-reduce | flops 8192 | bytes 32768
  61.2 66.7 %all-gather = bf16[32,1,128]{2,1,0:T(2,128)(2,1)S(1)} all-gather(bf16[1,1,128]{2,1,0:T(2,128)(2,1)} %bitcast.268), channel_id=1, replica_groups=mesh['dev'=8,'rep'=4] {'dev','rep'}, dimensions={0}, use_global_device_ids=true | all-gather | bytes 8448 | tf_op jit(solution)/shard_map/all_gather | solution.py:226
  127.9 6.5 fusion.128
  137.8 3.3 fusion.127
  141.0 2.2 convert_reduce_fusion.7
  143.3 2.3 convert_reduce_fusion.6
  145.6 8.8 add_convert_fusion.3
  154.4 6.2 copy.72
  160.5 13.8 multiply_reduce_fusion.3
  174.3 10.6 fusion
  185.6 15.9 %fusion.69 = bf16[16,64,577]{2,1,0:T(8,128)(2,1)} fusion(f32[16,577,577]{1,2,0:T(8,128)} %get-tuple-element.224, f32[16,577]{1,0:T(8,128)S(1)} %fusion, f32[16,577]{1,0:T(8,128)S(1)} %get-tuple-element.223, bf16[1,577,3,16,64]{1,4,3,2,0:T(8,128)(2,1)} %bitcast.246), kind=kOutput, calls=%fused_computation.147 | convolution fusion | flops 703736896 | bytes 26486912 | tf_op jit(solution)/shard_map/while/body/eval_jaxpr/hqk,khd->qhd/dot_general | solution.py:41
  201.5 6.3 add_convert_fusion.2
  207.8 6.2 copy.75
  213.9 13.6 multiply_reduce_fusion.2
  227.5 10.9 fusion.1
  239.1 14.7 fusion.68
  253.8 4.1 fusion.133
  259.1 1.6 fusion.134
  262.6 8.9 fusion.118
  271.6 3.7 copy-done.80
  275.3 52.1 %multiply_convert_fusion.3 = (bf16[577,4096]{1,0:T(8,128)(2,1)}, f32[577,4096]{1,0:T(8,128)}, bf16[577,4096]{1,0:T(8,128)(2,1)}, f32[577,4096]{1,0:T(8,128)}, f32[577,4096]{1,0:T(8,128)}) fusion(f32[4096]{0:T(1024)S(1)} %bitcast.265, f32[577,4096]{1,0:T(8,128)S(1)} %fusion.118, bf16[1024,4096]{1,0:T(8,128)(2,1)S(1)} %copy-done.75, ...), kind=kOutput, calls=%fused_computation.45 | convolution fusion | flops 5155148800 | bytes 58049032 | tf_op jit(solution)/shard_map/dot_general | solution.py:108
  327.4 17.2 %convert_reduce_fusion = (f32[4096]{0:T(1024)}, bf16[577,4096]{1,0:T(8,128)(2,1)}) fusion(f32[577,4096]{1,0:T(8,128)} %get-tuple-element.208, bf16[4096,1024]{1,0:T(8,128)(2,1)} %all-gather.12.cloned.1.call-done, bf16[1,577,1024]{2,1,0:T(8,128)(2,1)} %get-tuple-element.176, f32[]{:T(128)} %bitcast.29, f32[577,4096]{1,0:T(8,128)} %copy-done.80, ...), kind=kOutput, calls=%fused_computation.28 | convolution fusion | flops 4882172928 | bytes 33236996 | tf_op jit(solution)/shard_map/dot_general | solution.py:30
  344.6 10.2 fusion.135
  354.8 17.5 %convert_reduce_fusion.1 = (f32[4096]{0:T(1024)}, bf16[577,4096]{1,0:T(8,128)(2,1)}) fusion(f32[577,4096]{1,0:T(8,128)} %get-tuple-element.192, bf16[4096,1024]{1,0:T(8,128)(2,1)} %all-gather.12.cloned.1.call-done, bf16[1,577,1024]{2,1,0:T(8,128)(2,1)S(1)} %copy-done.15, f32[]{:T(128)} %bitcast.18, f32[577,4096]{1,0:T(8,128)} %get-tuple-element.229, ...), kind=kOutput, calls=%fused_computation.29 | convolution fusion | flops 4882172928 | bytes 33236996 | tf_op jit(solution)/shard_map/dot_general | solution.py:30
  372.3 12.2 multiply_reduce_fusion.5
  384.6 2.2 fusion.123
  389.4 2.5 convolution_convert_fusion
  391.9 2.8 copy.83
  394.7 13.5 fusion.65
  408.2 15.7 %multiply_reduce_fusion = (f32[16,577]{1,0:T(8,128)S(1)}, f32[16,577,577]{1,2,0:T(8,128)}) fusion(f32[16,577,577]{1,2,0:T(8,128)} %get-tuple-element.222, f32[16,577]{1,0:T(8,128)S(1)} %copy-done.31, bf16[577,16,64]{0,2,1:T(8,128)(2,1)} %bitcast.258, bf16[1,577,3,16,64]{1,4,3,2,0:T(8,128)(2,1)} %bitcast.252), kind=kOutput, calls=%fused_computation.1 | convolution fusion | flops 703136768 | bytes 47923392 | tf_op jit(solution)/shard_map/while/body/eval_jaxpr/qhd,khd->hqk/dot_general | solution.py:52
  424.0 3.1 convert_reduce_fusion.9
  427.1 3.9 fusion.136
  431.0 2.5 convolution_convert_fusion.1
  433.5 2.4 copy.78
  435.9 6.9 convolution_add_fusion.3
  442.9 20.5 %multiply_convert_fusion = bf16[16,577,577]{1,2,0:T(8,128)(2,1)} fusion(f32[16,577,577]{1,2,0:T(8,128)} %get-tuple-element.232, f32[16,577,577]{1,2,0:T(8,128)} %get-tuple-element.222, f32[16,577]{1,0:T(8,128)S(1)} %get-tuple-element.231, f32[16,577]{1,0:T(8,128)S(1)} %copy-done.31), kind=kLoop, calls=%fused_computation | loop fusion | flops 26634320 | bytes 53342496 | tf_op jit(solution)/shard_map/while/body/eval_jaxpr/convert_element_type | solution.py:54
  463.3 9.5 multiply_bitcast_fusion
  472.9 16.0 %multiply_reduce_fusion.1 = (f32[16,577]{1,0:T(8,128)S(1)}, f32[16,577,577]{1,2,0:T(8,128)}) fusion(f32[16,577,577]{1,2,0:T(8,128)} %get-tuple-element.224, f32[16,577]{1,0:T(8,128)S(1)} %copy-done.30, bf16[577,16,64]{0,2,1:T(8,128)(2,1)} %bitcast.255, bf16[1,577,3,16,64]{1,4,3,2,0:T(8,128)(2,1)} %bitcast.247), kind=kOutput, calls=%fused_computation.4 | convolution fusion | flops 703136768 | bytes 47923392 | tf_op jit(solution)/shard_map/while/body/eval_jaxpr/qhd,khd->hqk/dot_general | solution.py:52
  488.8 7.2 multiply_bitcast_fusion.1
  496.1 4.5 convert_reduce_fusion.2
  500.5 2.3 copy-done
  502.8 15.2 %multiply_convert_fusion.1 = bf16[16,577,577]{1,2,0:T(8,128)(2,1)} fusion(f32[16,577,577]{1,2,0:T(8,128)S(1)} %copy-done, f32[16,577,577]{1,2,0:T(8,128)} %get-tuple-element.224, f32[16,577]{1,0:T(8,128)S(1)} %get-tuple-element.233, f32[16,577]{1,0:T(8,128)S(1)} %copy-done.30), kind=kLoop, calls=%fused_computation.3 | loop fusion | flops 26634320 | bytes 53342496 | tf_op jit(solution)/shard_map/while/body/eval_jaxpr/convert_element_type | solution.py:54
  518.0 9.1 multiply_bitcast_fusion.2
  527.1 7.8 multiply_bitcast_fusion.3
  534.9 13.5 fusion.62
  548.4 2.6 convert_reduce_fusion.3
  551.1 8.9 fusion.79
  560.0 12.2 convolution_add_fusion.2
  572.9 13.1 fusion.116
  586.0 15.5 %convolution_add_fusion = f32[1024,4096]{1,0:T(8,128)} fusion(f32[1024,4096]{1,0:T(8,128)} %fusion.116, bf16[577,4096]{1,0:T(8,128)(2,1)} %get-tuple-element.240, f32[577,1024]{1,0:T(8,128)S(1)} %copy-done.20, f32[577]{0:T(1024)S(1)} %copy-done.67, f32[577]{0:T(1024)S(1)} %copy-done.56, f32[1024]{0:T(1024)S(1)} %copy-done.33, ...), kind=kOutput, calls=%fused_computation.64 | convolution fusion | flops 4847375360 | bytes 40657416 | tf_op jit(solution)/shard_map/dot_general | solution.py:24
  601.5 12.9 fusion.103
  614.5 15.8 %convolution_add_fusion.1 = f32[4096,1024]{1,0:T(8,128)} fusion(f32[4096,1024]{1,0:T(8,128)} %fusion.103, bf16[577,4096]{1,0:T(8,128)(2,1)} %get-tuple-element.207, bf16[1,577,1024]{2,1,0:T(8,128)(2,1)S(1)} %copy-done.14, f32[]{:T(128)} %bitcast.29), kind=kOutput, calls=%fused_computation.67 | convolution fusion | flops 4846193664 | bytes 39462916 | tf_op jit(solution)/shard_map/dot_general | solution.py:24
  631.0 9.6 fusion.70
  640.6 9.2 fusion.71
  650.1 3.8 copy.87
  654.3 8.2 fusion.120
  662.6 8.9 fusion.44
  671.6 3.1 fusion.47
  674.7 39.8 %all-reduce.15 = (f32[1024]{0:T(1024)S(1)}, f32[1024]{0:T(1024)S(1)}, f32[2048]{0:T(1024)S(1)}, f32[1024]{0:T(1024)S(1)}, f32[1024]{0:T(1024)S(1)}, /*index=5*/f...) all-reduce(f32[1024]{0:T(1024)S(1)} %add.317, ...), channel_id=14, replica_groups=mesh['dev'=8,'rep'=4] {'dev','rep'}, use_global_device_ids=true, to_apply=%region_23.24.clone | all-reduce | flops 12288 | bytes 98304
  718.0 3.1 fusion.75
  721.4 3.8 copy.88
  726.4 23.6 %reduce-scatter.5.cloned.1.call-done = f32[32,3072]{1,0:T(8,128)} async-done(((f32[1024,3072]{1,0:T(8,128)}), f32[32,3072]{1,0:T(8,128)}) %reduce-scatter.5.cloned.1.call-update) | async-done | bytes 393232 | tf_op jit(solution)/shard_map/reduce_scatter | solution.py:301
  750.0 366.3 %reduce-scatter.9.cloned.1.call-done = f32[32,4096]{1,0:T(8,128)} async-done(((f32[1024,4096]{1,0:T(8,128)}), f32[32,4096]{1,0:T(8,128)}) %reduce-scatter.9.cloned.1.call-update) | async-done | bytes 524304 | tf_op jit(solution)/shard_map/reduce_scatter | solution.py:307
  1116.3 365.2 %reduce-scatter.11.cloned.1.call-done = f32[128,1024]{1,0:T(8,128)} async-done(((f32[4096,1024]{1,0:T(8,128)}), f32[128,1024]{1,0:T(8,128)}) %reduce-scatter.11.cloned.1.call-update) | async-done | bytes 524304 | tf_op jit(solution)/shard_map/reduce_scatter | solution.py:309
  (259 shorter events, 27.4 us)
Async XLA Ops:
  7.2 138.4 %all-gather.6.cloned.1.call-start = ((), (), s32[]{:S(2)}) async-start(), calls=%async_computation.4 | async-start | bytes 6488064 | tf_op jit(solution)/shard_map/all_gather | solution.py:219
  7.9 245.9 %all-gather.8.cloned.1.call-start = ((), (), s32[]{:S(2)}) async-start(), calls=%async_computation.5 | async-start | bytes 2162688 | tf_op jit(solution)/shard_map/all_gather | solution.py:221
  8.7 253.9 %all-gather.10.cloned.1.call-start = ((), (), s32[]{:S(2)}) async-start(), calls=%async_computation.6 | async-start | bytes 8650752 | tf_op jit(solution)/shard_map/all_gather | solution.py:225
  9.4 318.0 %all-gather.12.cloned.1.call-start = ((), (), s32[]{:S(2)}) async-start(), calls=%async_computation.7 | async-start | bytes 8650752 | tf_op jit(solution)/shard_map/all_gather | solution.py:227
  10.0 716.4 %reduce-scatter.7.cloned.1.call-start = ((), (), s32[]{:S(2)}) async-start(), calls=%async_computation.9 | async-start | bytes 4325376 | tf_op jit(solution)/shard_map/reduce_scatter | solution.py:303
  61.1 140.3 %copy-start.36 = (f32[1024]{0:T(1024)}, f32[1024]{0:T(1024)S(1)}, u32[]{:S(2)}) copy-start(f32[1024]{0:T(1024)S(1)} %convert_element_type.257) | copy-start | bytes 12292
  61.1 140.3 %copy-start.72 = (f32[1024]{0:T(1024)}, f32[1024]{0:T(1024)S(1)}, u32[]{:S(2)}) copy-start(f32[1024]{0:T(1024)S(1)} %convert_element_type.258) | copy-start | bytes 12292
  61.1 210.5 %copy-start.32 = (f32[1024]{0:T(1024)}, f32[1024]{0:T(1024)S(1)}, u32[]{:S(2)}) copy-start(f32[1024]{0:T(1024)S(1)} %convert_element_type.268) | copy-start | bytes 12292
  135.2 10.4 copy-start.9
  135.2 66.2 %copy-start.5 = (bf16[1,577,1024]{2,1,0:T(8,128)(2,1)}, bf16[1,577,1024]{2,1,0:T(8,128)(2,1)S(1)}, u32[]{:S(2)}) copy-start(bf16[1,577,1024]{2,1,0:T(8,128)(2,1)S(1)} %get-tuple-element.198) | copy-start | bytes 3545092
  135.2 66.2 %copy-start.34 = (f32[577]{0:T(1024)}, f32[577]{0:T(1024)S(1)}, u32[]{:S(2)}) copy-start(f32[577]{0:T(1024)S(1)} %broadcast_multiply_fusion.1) | copy-start | bytes 6928
  135.3 10.3 copy-start.40
  136.3 9.3 copy-start.57
  136.8 4.3 copy-start.46
  137.8 63.7 %copy-start.38 = (f32[577]{0:T(1024)}, f32[577]{0:T(1024)S(1)}, u32[]{:S(2)}) copy-start(f32[577]{0:T(1024)S(1)} %fusion.108) | copy-start | bytes 6928
  174.3 27.2 %slice-start = ((s8[6291456]{0:T(1024)(128)(4,1)}), s8[4194304]{0:T(1024)(128)(4,1)S(1)}, s32[]{:S(2)}) async-start(s8[6291456]{0:T(1024)(128)(4,1)} %bitcast.269), calls=%async_computation.12 | async-start | bytes 8388608
  185.6 15.9 %slice-start.1 = ((s8[6291456]{0:T(1024)(128)(4,1)}), s8[2097152]{0:T(1024)(128)(4,1)S(1)}, s32[]{:S(2)}) async-start(s8[6291456]{0:T(1024)(128)(4,1)} %bitcast.269), calls=%async_computation.13 | async-start | bytes 4194304
  253.8 4.5 copy-start.25
  253.8 4.5 copy-start.76
  260.8 10.8 copy-start.54
  262.5 9.0 copy-start.52
  262.6 9.0 copy-start.65
  262.6 12.7 copy-start.75
  344.6 10.2 copy-start.15
  354.8 17.5 %copy-start.19 = (f32[577,1024]{1,0:T(8,128)S(1)}, f32[577,1024]{1,0:T(8,128)}, u32[]{:S(2)}) copy-start(f32[577,1024]{1,0:T(8,128)} %copy-done.18) | copy-start | bytes 7090180
  354.8 17.5 %copy-start.55 = (f32[577]{0:T(1024)S(1)}, f32[577]{0:T(1024)}, u32[]{:S(2)}) copy-start(f32[577]{0:T(1024)} %copy-done.54) | copy-start | bytes 6928
  354.8 17.5 %copy-start.66 = (f32[577]{0:T(1024)S(1)}, f32[577]{0:T(1024)}, u32[]{:S(2)}) copy-start(f32[577]{0:T(1024)} %copy-done.65) | copy-start | bytes 6928
  372.3 12.2 copy-start.53
  372.3 12.2 copy-start.51
  372.3 12.2 copy-start.29
  442.8 307.2 %reduce-scatter.5.cloned.1.call-start = ((), (), s32[]{:S(2)}) async-start(), calls=%async_computation.8 | async-start | bytes 12976128 | tf_op jit(solution)/shard_map/reduce_scatter | solution.py:301
  463.3 9.5 copy-start.30
  488.8 14.0 copy-start
  502.8 15.2 %copy-start.1 = (bf16[577,3072]{0,1:T(8,128)(2,1)S(1)}, bf16[577,3072]{0,1:T(8,128)(2,1)}, u32[]{:S(2)}) copy-start(bf16[577,3072]{0,1:T(8,128)(2,1)} %copy.72) | copy-start | bytes 10635268
  551.0 9.0 copy-start.28
  551.1 8.9 copy-start.7
  551.1 8.9 copy-start.26
  551.1 8.9 copy-start.35
  551.1 8.9 copy-start.39
  572.2 13.7 copy-start.56
  572.2 13.7 copy-start.67
  572.3 544.0 %reduce-scatter.9.cloned.1.call-start = ((), (), s32[]{:S(2)}) async-start(), calls=%async_computation.10 | async-start | bytes 17301504 | tf_op jit(solution)/shard_map/reduce_scatter | solution.py:307
  572.9 13.1 copy-start.20
  601.5 880.0 %reduce-scatter.11.cloned.1.call-start = ((), (), s32[]{:S(2)}) async-start(), calls=%async_computation.11 | async-start | bytes 17301504 | tf_op jit(solution)/shard_map/reduce_scatter | solution.py:309
  601.5 12.9 copy-start.14
  631.0 9.6 copy-start.21
  650.0 4.2 copy-start.61
  650.0 4.2 copy-start.62
  650.0 4.2 copy-start.70
  650.0 4.2 copy-start.68
  650.0 4.2 copy-start.69
  650.0 4.2 copy-start.59
  650.0 4.2 copy-start.60
  650.1 4.3 copy-start.11
  654.3 8.2 copy-start.49
  654.3 8.2 copy-start.8
  654.3 8.2 copy-start.27
  662.6 8.9 copy-start.47
  662.6 9.0 copy-start.2
  662.6 9.0 copy-start.12
  662.6 9.0 copy-start.16
  662.6 9.0 copy-start.45
  671.6 46.4 %copy-start.4 = (f32[577,1024]{1,0:T(8,128)S(1)}, f32[577,1024]{1,0:T(8,128)}, u32[]{:S(2)}) copy-start(f32[577,1024]{1,0:T(8,128)} %copy-done.3) | copy-start | bytes 7090180
  671.6 46.4 %copy-start.43 = (f32[577]{0:T(1024)S(1)}, f32[577]{0:T(1024)}, u32[]{:S(2)}) copy-start(f32[577]{0:T(1024)} %copy-done.42) | copy-start | bytes 6928
  (27 other events, 60.5 us)
Sparse Core Ops, SparseCore 0:
  10.9 72.3 all-gather.5
  86.2 55.2 all-gather.7
  144.4 76.2 all-gather.9
  223.5 76.0 all-gather.11
  442.9 145.8 reduce-scatter.6
  595.2 154.6 reduce-scatter.4
  752.9 363.3 reduce-scatter.8
  1119.3 362.1 reduce-scatter.10
where the time goes:
time: 1490 us
  waiting for transfers between devices  758 us (51%)
  matrix products  419 us (28%)
  blocking collectives  149 us (10%)
  other arithmetic  85.8 us (6%)
  local copies, waits for them, and re-layouts  59.9 us (4%)
  between operations  16.9 us (1%)
    reduce_scatter x1, waiting for transfers between devices, body(): lax.psum_scatter(grads[8], ('dev', 'rep'), scatter_dimension=0, tiled=True)  366 us
    reduce_scatter x1, waiting for transfers between devices, body(): lax.psum_scatter(grads[10], ('dev', 'rep'), scatter_dimension=0, tiled=True)  365 us
    dot_general x8, matrix products, inner_rows(): lax.dot_general(left, right, (((0,), (0,)), ((), ())), preferred_element_...  89.2 us
    unnamed x2, blocking collectives  82.3 us
    dot_general x8, matrix products, times_trans(): lax.dot_general(left, right, (((1,), (1,)), ((), ())), preferred_element_...  79 us
    all_gather x1, blocking collectives, fetch_forward(): lax.all_gather(shards[9], ('dev', 'rep'), axis=0, tiled=True)  66.7 us
    dot_general x2, matrix products, run_forward(): jnp.dot(normed_two, up_mat, preferred_element_type=jnp.float32)  61 us
    convert_element_type x2, other arithmetic, attend_back(): score_low = score_grad.astype(jnp.bfloat16)  35.6 us
  transfers between devices with their start and end apart: 8, of which 3 were waited for; matrix products, arithmetic and copies ran while one was open for 29% of the time, Pallas kernels for 0%

commit v1 on v0

v1 whole, which is shorter than its diff:
```python
import functools
import math

import jax
import jax.numpy as jnp
from jax import lax
from jax.experimental import pallas as pl
from jax.experimental.pallas import tpu as pltpu
from jax.sharding import PartitionSpec as P

HEADS = 16
HD = 64
LANES = 128
EPS = 1e-06
AXES = ("dev", "rep")
BF = jnp.bfloat16
F32 = jnp.float32


def mm(left, right):
    return jnp.dot(left, right, preferred_element_type=F32)


def mm_nt(left, right):
    return lax.dot_general(left, right, (((1,), (1,)), ((), ())), preferred_element_type=F32)


def mm_tn(left, right):
    return lax.dot_general(left, right, (((0,), (0,)), ((), ())), preferred_element_type=F32)


def head_masks(shape):
    lane = lax.broadcasted_iota(jnp.int32, shape, 1)
    return [(lane >= h * HD) & (lane < (h + 1) * HD) for h in range(LANES // HD)]


def attend_kernel(seq, scale, q_ref, k_ref, v_ref, out_ref, log_ref):
    queries = q_ref[...]
    keys = k_ref[...] * jnp.asarray(scale, BF)
    values = v_ref[...]
    rows = queries.shape[0]
    masks = head_masks(queries.shape)
    zero = jnp.zeros((), BF)
    total = None
    for h, mask in enumerate(masks):
        scores = mm_nt(jnp.where(mask, keys, zero), queries)
        row = lax.broadcasted_iota(jnp.int32, scores.shape, 0)
        scores = jnp.where(row < seq, scores, -1e30)
        highest = jnp.max(scores, axis=0, keepdims=True)
        raised = jnp.exp(scores - highest)
        sums = jnp.sum(raised, axis=0, keepdims=True)
        probs = (raised * (1.0 / sums)).astype(BF)
        mixed = mm_tn(probs, jnp.where(mask, values, zero))
        total = mixed if total is None else total + mixed
        log_ref[0, 0, h : h + 1, :] = highest + jnp.log(sums)
    out_ref[...] = total.astype(BF)


def attend_back_kernel(seq, scale, q_ref, k_ref, v_ref, g_ref, log_ref, dq_ref, dk_ref, dv_ref):
    queries = q_ref[...]
    keys = k_ref[...] * jnp.asarray(scale, BF)
    values = v_ref[...]
    grads = g_ref[...]
    masks = head_masks(queries.shape)
    zero = jnp.zeros((), BF)
    dq = dk = dv = None
    for h, mask in enumerate(masks):
        key_own = jnp.where(mask, keys, zero)
        scores = mm_nt(key_own, queries)
        row = lax.broadcasted_iota(jnp.int32, scores.shape, 0)
        probs = jnp.where(row < seq, jnp.exp(scores - log_ref[0, 0, h : h + 1, :]), 0.0)
        prob_grad = mm_nt(jnp.where(mask, values, zero), grads)
        share = jnp.sum(probs * prob_grad, axis=0, keepdims=True)
        score_low = (probs * (prob_grad - share)).astype(BF)
        dv_h = mm(probs.astype(BF), jnp.where(mask, grads, zero))
        dk_h = mm(score_low, jnp.where(mask, queries, zero))
        dq_h = mm_tn(score_low, key_own)
        dv = dv_h if dv is None else dv + dv_h
        dk = dk_h if dk is None else dk + dk_h
        dq = dq_h if dq is None else dq + dq_h
    dq_ref[...] = dq.astype(BF)
    dk_ref[...] = (dk * scale).astype(BF)
    dv_ref[...] = dv.astype(BF)


def attend(joined, images_now, rows, seq, scale):
    width = joined.shape[1] // 3
    pairs = width // LANES

    def part(which):
        return pl.BlockSpec((rows, LANES), lambda i, j: (i, which * pairs + j))

    heads = LANES // HD
    return pl.pallas_call(
        functools.partial(attend_kernel, seq, scale),
        grid=(images_now, pairs),
        in_specs=[part(0), part(1), part(2)],
        out_specs=[
            pl.BlockSpec((rows, LANES), lambda i, j: (i, j)),
            pl.BlockSpec((1, 1, heads, rows), lambda i, j: (i, j, 0, 0)),
        ],
        out_shape=[
            jax.ShapeDtypeStruct((images_now * rows, width), BF),
            jax.ShapeDtypeStruct((images_now, pairs, heads, rows), F32),
        ],
        compiler_params=pltpu.CompilerParams(vmem_limit_bytes=40 << 20),
        cost_estimate=pl.CostEstimate(
            flops=4 * images_now * HEADS * rows * rows * LANES * 2,
            bytes_accessed=images_now * rows * width * 8,
            transcendentals=images_now * HEADS * rows * rows,
        ),
        name="attend",
    )(joined, joined, joined)


def attend_back(joined, grads, logs, images_now, rows, seq, scale):
    width = joined.shape[1] // 3
    pairs = width // LANES
    heads = LANES // HD

    def part(which):
        return pl.BlockSpec((rows, LANES), lambda i, j: (i, which * pairs + j))

    own = pl.BlockSpec((rows, LANES), lambda i, j: (i, j))
    return pl.pallas_call(
        functools.partial(attend_back_kernel, seq, scale),
        grid=(images_now, pairs),
        in_specs=[
            part(0),
            part(1),
            part(2),
            own,
            pl.BlockSpec((1, 1, heads, rows), lambda i, j: (i, j, 0, 0)),
        ],
        out_specs=[own, own, own],
        out_shape=[jax.ShapeDtypeStruct((images_now * rows, width), BF)] * 3,
        compiler_params=pltpu.CompilerParams(vmem_limit_bytes=48 << 20),
        cost_estimate=pl.CostEstimate(
            flops=10 * images_now * HEADS * rows * rows * LANES * 2,
            bytes_accessed=images_now * rows * width * 14,
            transcendentals=images_now * HEADS * rows * rows,
        ),
        name="attend_back",
    )(joined, joined, joined, grads, logs)


def index_bits(sizes):
    dev, rep = sizes
    out = []
    for size, stride, axis in ((dev, rep, "dev"), (rep, 1, "rep")):
        for bit in reversed(range(size.bit_length() - 1)):
            step = stride << bit
            out.append((axis, bit, [(i, i ^ step) for i in range(dev * rep)]))
    return out


def scatter_sum(full, sizes, orders):
    bits = index_bits(sizes)
    count = sizes[0] * sizes[1]
    rows = full.shape[0] // count
    pieces = []
    cut = full.shape[1] // len(orders)
    for number, order in enumerate(orders):
        value = full[:, number * cut : (number + 1) * cut]
        value = value.reshape((2,) * len(bits) + (rows, cut))
        left = list(range(len(bits)))
        for which in order:
            axis, bit, flips = bits[which]
            place = left.index(which)
            mine = (lax.axis_index(axis) >> bit) & 1
            send = lax.dynamic_index_in_dim(value, 1 - mine, place, keepdims=False)
            keep = lax.dynamic_index_in_dim(value, mine, place, keepdims=False)
            value = keep + lax.ppermute(send, AXES, flips)
            left.remove(which)
        pieces.append(value.reshape(rows, cut))
    return jnp.concatenate(pieces, axis=1).astype(F32)


def norm_stats(values):
    centred = values - jnp.mean(values, axis=-1, keepdims=True)
    spread = jnp.mean(centred * centred, axis=-1, keepdims=True)
    inverse = lax.rsqrt(spread + EPS)
    return centred * inverse, inverse


def norm_back(normed, inverse, gain, grad):
    scaled = grad * gain
    return inverse * (
        scaled
        - jnp.mean(scaled, axis=-1, keepdims=True)
        - normed * jnp.mean(scaled * normed, axis=-1, keepdims=True)
    )


def gelu_and_slope(values):
    half = 0.5 * (1.0 + lax.erf(values * (1.0 / math.sqrt(2.0))))
    bell = jnp.exp(-0.5 * values * values) * (1.0 / math.sqrt(2.0 * math.pi))
    return values * half, half + values * bell


def body(sizes, *args):
    images, cotangent, filled = args[0], args[13], args[14]
    small_in = (args[1], args[2], args[4], args[6], args[7], args[8], args[10], args[12])
    big_in = (args[3], args[5], args[9], args[11])
    count = sizes[0] * sizes[1]
    images_now, seq, width = images.shape
    rows = -(-seq // 16) * 16
    tokens = images_now * rows
    scale = 1.0 / math.sqrt(HD)

    packed = lax.all_gather(jnp.concatenate(small_in), AXES, axis=0, tiled=False)
    packed = packed.reshape(count, -1)
    smalls, at = [], 0
    for one in small_in:
        smalls.append(packed[:, at : at + one.shape[0]].reshape(-1).astype(F32))
        at += one.shape[0]
    gain_one, bias_one, joint_bias, proj_bias, gain_two, bias_two, up_bias, down_bias = smalls
    joint_w, proj_w, up_w, down_w = [lax.all_gather(w, AXES, axis=0, tiled=True) for w in big_in]

    pad = ((0, 0), (0, rows - seq), (0, 0))
    residual_in = jnp.pad(images, pad).reshape(tokens, width).astype(F32)
    n_one, r_one = norm_stats(residual_in)
    normed_one = (n_one * gain_one + bias_one).astype(BF)
    bias_full = jnp.concatenate([joint_bias[:width], jnp.zeros((width,), F32), joint_bias[width:]])
    joined = (mm(normed_one, joint_w) + bias_full).astype(BF)
    heads_out, logs = attend(joined, images_now, rows, seq, scale)
    middle = residual_in + mm(heads_out, proj_w) + proj_bias
    n_two, r_two = norm_stats(middle)
    normed_two = (n_two * gain_two + bias_two).astype(BF)
    activated, slope = gelu_and_slope(mm(normed_two, up_w) + up_bias)
    activated = activated.astype(BF)
    slope = slope.astype(BF)
    output = (middle + mm(activated, down_w) + down_bias).astype(BF)
    output = output.reshape(images_now, rows, width)[:, :seq]

    flags = filled.astype(BF)[:, None, None]
    branch = jnp.pad(cotangent * flags, pad).reshape(tokens, width)
    out_grad = branch.astype(F32)
    orders = scatter_orders(sizes)
    down_grad = mm_tn(activated, branch).astype(BF)
    down_sum = scatter_sum(down_grad, sizes, orders)
    pre_grad = (mm_nt(branch, down_w) * slope).astype(BF)
    up_grad = mm_tn(normed_two, pre_grad).astype(BF)
    up_sum = scatter_sum(up_grad, sizes, orders)
    norm_two_in = mm_nt(pre_grad, up_w)
    middle_grad = out_grad + norm_back(n_two, r_two, gain_two, norm_two_in)
    attn_grad = middle_grad.astype(BF)
    proj_grad = mm_tn(heads_out, attn_grad).astype(BF)
    proj_sum = scatter_sum(proj_grad, sizes, orders)
    heads_grad = mm_nt(attn_grad, proj_w).astype(BF)
    dq, dk, dv = attend_back(joined, heads_grad, logs, images_now, rows, seq, scale)
    joined_grad = jnp.concatenate([dq, dk, dv], axis=1)
    joint_grad = mm_tn(normed_one, joined_grad).astype(BF)
    joint_sum = scatter_sum(joint_grad, sizes, orders)
    norm_one_in = mm_nt(joined_grad, joint_w)
    input_grad = (middle_grad + norm_back(n_one, r_one, gain_one, norm_one_in)).astype(BF)
    input_grad = input_grad.reshape(images_now, rows, width)[:, :seq]

    def over_tokens(value):
        return jnp.sum(value, axis=0, dtype=F32)

    joint_sums = over_tokens(joined_grad)
    small_grads = (
        over_tokens(norm_one_in * n_one),
        over_tokens(norm_one_in),
        jnp.concatenate([joint_sums[:width], joint_sums[2 * width :]]),
        over_tokens(attn_grad),
        over_tokens(norm_two_in * n_two),
        over_tokens(norm_two_in),
        over_tokens(pre_grad),
        over_tokens(branch),
    )
    stacked = jnp.concatenate([g.reshape(count, -1) for g in small_grads], axis=1)
    mine = lax.psum_scatter(stacked, AXES, scatter_dimension=0, tiled=True).reshape(-1)
    shares, at = [], 0
    for one in small_in:
        shares.append(mine[at : at + one.shape[0]])
        at += one.shape[0]
    return (
        output,
        input_grad,
        shares[0],
        shares[1],
        joint_sum,
        shares[2],
        proj_sum,
        shares[3],
        shares[4],
        shares[5],
        up_sum,
        shares[6],
        down_sum,
        shares[7],
    )


def scatter_orders(sizes):
    bits = len(index_bits(sizes))
    devs = sizes[0].bit_length() - 1
    reps = list(range(devs, bits))
    if devs < 3:
        return [list(range(bits))] * 2
    inner = list(range(devs - 3))
    y, x, core = devs - 3, devs - 2, devs - 1
    return [[core, x, y] + inner + reps, [core, y, x] + inner + reps]


def solution(mesh):
    sizes = (mesh.shape["dev"], mesh.shape["rep"])
    both = ("dev", "rep")
    three, one, two = P(both, None, None), P(both), P(both, None)
    in_specs = (three, one, one, two, one, two, one, one, one, two, one, two, one, three, one)
    out_specs = (three, three, one, one, two, one, two, one, one, one, two, one, two, one)
    return jax.shard_map(
        functools.partial(body, sizes),
        mesh=mesh,
        in_specs=in_specs,
        out_specs=out_specs,
        check_vma=False,
    )
```

time: 1490 us -> 816 us (0.55)
  waiting for transfers between devices: 758 us -> 292 us
  matrix products: 419 us -> 162 us
  Pallas kernels: 0 us -> 85.4 us
  blocking collectives: 149 us -> 111 us
  other arithmetic: 85.8 us -> 52.3 us
  starting transfers between devices: 0.32 us -> 29.5 us
    reduce_scatter x4 -> x0, waiting for transfers between devices: 755 us -> none  [the longest x1 366 us: body(): lax.psum_scatter(grads[8], ('dev', 'rep'), scatter_dimension=0, tiled=True)]
    dot_general x36 -> x12, matrix products: 419 us -> 162 us  [the longest x4 61.2 us: mm_nt(): lax.dot_general(left, right, (((1,), (1,)), ((), ())), preferred_element_...]
    ppermute x0 -> x40, waiting for transfers between devices: none -> 194 us  [scatter_sum(): value = keep + lax.ppermute(send, AXES, flips)]
    all_gather x4, waiting for transfers between devices: 0.03 us -> 95.3 us  [body(): lax.all_gather(w, AXES, axis=0, tiled=True)]
    pallas_call x0 -> x2, Pallas kernels: none -> 85.4 us  [the longest x1 50.4 us: attend_back(): pl.pallas_call(functools.partial(attend_back_kernel, seq, scale), grid=(i...]
    unnamed x2 -> x1, blocking collectives: 82.3 us -> 39.7 us
    ppermute x0 -> x40, starting transfers between devices: none -> 29.4 us  [scatter_sum(): value = keep + lax.ppermute(send, AXES, flips)]
    convert_element_type x9 -> x10, other arithmetic: 35.7 us -> 12.5 us  [the longest x1 6.39 us: body(): (middle_grad + norm_back(n_one, r_one, gain_one, norm_one_in)).astype(BF)]
  transfers between devices with their start and end apart: 8 -> 44, of which waited for: 3 -> 28; matrix products, arithmetic and copies ran while one was open for 29% -> 17% of each run, Pallas kernels for 0% -> 4%
where the time goes in v1:
time: 816 us; the launch traced here: 812 us
  waiting for transfers between devices  292 us (36%)
  matrix products  162 us (20%)
  blocking collectives  111 us (14%)
  Pallas kernels  85.4 us (10%)
  local copies, waits for them, and re-layouts  65.4 us (8%)
  other arithmetic  52.3 us (6%)
  starting transfers between devices  29.5 us (4%)
  between operations  15 us (2%)
    ppermute x40, waiting for transfers between devices, scatter_sum(): value = keep + lax.ppermute(send, AXES, flips)  194 us
    all_gather x4, waiting for transfers between devices, body(): lax.all_gather(w, AXES, axis=0, tiled=True)  95.3 us
    all_gather x1, blocking collectives, body(): lax.all_gather(jnp.concatenate(small_in), AXES, axis=0, tiled=False)  70.9 us
    dot_general x4, matrix products, mm_nt(): lax.dot_general(left, right, (((1,), (1,)), ((), ())), preferred_element_...  61.2 us
    dot_general x4, matrix products, mm(): return jnp.dot(left, right, preferred_element_type=F32)  53.4 us
    pallas_call x1, Pallas kernels, attend_back(): pl.pallas_call(functools.partial(attend_back_kernel, seq, scale), grid=(i...  50.4 us
    dot_general x4, matrix products, mm_tn(): lax.dot_general(left, right, (((0,), (0,)), ((), ())), preferred_element_...  47.9 us
    unnamed x1, blocking collectives  39.7 us
  transfers between devices with their start and end apart: 44, of which 28 were waited for; matrix products, arithmetic and copies ran while one was open for 17% of the time, Pallas kernels for 4%

profile of v1, /device:TPU:0, one launch (start us, length us, event | category | flops | bytes accessed | tf_op | source)
XLA Modules:
  0.0 812.4 jit_solution(932628934730335175)
XLA Ops:
  10.7 5.4 concatenate.32
  16.1 70.9 %all-gather.1 = bf16[32,1,384]{2,1,0:T(2,128)(2,1)S(1)} all-gather(bf16[1,1,384]{2,1,0:T(2,128)(2,1)S(1)} %reshape.260), channel_id=2, replica_groups=mesh['dev'=8,'rep'=4] {'dev','rep'}, dimensions={0}, use_global_device_ids=true | all-gather | bytes 25344 | tf_op jit(solution)/shard_map/all_gather | solution.py:211
  88.4 4.2 convert_reduce_fusion.4
  92.7 8.7 %multiply_reduce_fusion.5 = f32[2,592]{0,1:T(8,128)S(1)} fusion(f32[2,592]{0,1:T(8,128)S(1)} %broadcast_multiply_fusion.1, bf16[2,577,1024]{2,0,1:T(2,128)(2,1)S(1)} %copy-done.2), kind=kLoop, calls=%fused_computation.32 | loop fusion | flops 4848480 | bytes 2372864 | tf_op jit(solution)/shard_map/reduce_sum | solution.py:181
  101.8 3.8 broadcast_multiply_fusion
  105.6 2.1 copy.57
  107.7 2.5 convert_reduce_fusion.2
  110.9 2.1 pad_convert_fusion
  113.0 3.7 copy.44
  119.9 2.7 fusion.6
  122.6 11.5 %add_convert_fusion.q_ref.k_ref.v_ref = bf16[1184,3072]{1,0:T(8,128)(2,1)S(1)} fusion(bf16[1024,3072]{1,0:T(8,128)(2,1)} %all-gather.7.cloned.1.call-done, f32[3072]{0:T(1024)S(1)} %pad_maximum_fusion.1, f32[1184,1024]{1,0:T(8,128)} %fusion.6, f32[1024]{0:T(1024)S(1)} %reshape.253, f32[1024]{0:T(1024)S(1)} %reshape.252), kind=kOutput, calls=%fused_computation.13 | convolution fusion | flops 7459995648 | bytes 18436096 | tf_op jit(solution)/shard_map/dot_general | solution.py:21
  134.1 35.0 %attend.1 = (bf16[1184,1024]{1,0:T(8,128)(2,1)S(1)}, f32[2,8,2,592]{3,2,1,0:T(2,128)S(1)}) custom-call(bf16[1184,3072]{1,0:T(8,128)(2,1)S(1)} %add_convert_fusion.q_ref.k_ref.v_ref, bf16[1184,3072]{1,0:T(8,128)(2,1)S(1)} %add_convert_fusion.q_ref.k_ref.v_ref, bf16[1184,3072]{1,0:T(8,128)(2,1)S(1)} %add_convert_fusion.q_ref.k_ref.v_ref), custom_call_target="tpu_custom_call" | custom-call | flops 11484004352 | bytes 9699328 | tf_op jit(solution)/shard_map/attend/pallas_call | solution.py:94
  169.0 2.9 copy-done
  172.0 6.6 fusion.7
  178.6 2.7 reduce_sum.146
  181.3 3.0 multiply_reduce_fusion.4
  184.3 36.4 %all-gather.11.cloned.1.call-done = bf16[1024,4096]{1,0:T(8,128)(2,1)} async-done(((bf16[32,4096]{1,0:T(8,128)(2,1)}), bf16[1024,4096]{1,0:T(8,128)(2,1)}) %all-gather.11.cloned.1.call-update) | async-done | bytes 8388624 | tf_op jit(solution)/shard_map/all_gather | solution.py:218
  220.7 19.8 %multiply_convert_fusion = (bf16[1184,4096]{1,0:T(8,128)(2,1)}, f32[1184,4096]{1,0:T(8,128)}) fusion(f32[4096]{0:T(1024)S(1)} %fusion.8, bf16[1024,4096]{1,0:T(8,128)(2,1)} %all-gather.11.cloned.1.call-done, f32[1184,1024]{1,0:T(8,128)} %fusion.7, f32[1024]{0:T(1024)S(1)} %reshape.256, f32[1024]{0:T(1024)S(1)} %reshape.255, f32[1184]{0:T(1024)S(1)} %add_rsqrt_fusion.1, ...), kind=kOutput, calls=%fused_computation.8 | convolution fusion | flops 9967271936 | bytes 42370304 | tf_op jit(solution)/shard_map/dot_general | solution.py:21
  240.5 59.0 %all-gather.13.cloned.1.call-done = bf16[4096,1024]{1,0:T(8,128)(2,1)} async-done(((bf16[128,1024]{1,0:T(8,128)(2,1)}), bf16[4096,1024]{1,0:T(8,128)(2,1)}) %all-gather.13.cloned.1.call-update) | async-done | bytes 8388624 | tf_op jit(solution)/shard_map/all_gather | solution.py:218
  299.5 22.5 %convert_reduce_fusion = (f32[4096]{0:T(1024)}, bf16[1184,4096]{1,0:T(8,128)(2,1)}) fusion(f32[1184,4096]{1,0:T(8,128)} %get-tuple-element.59, bf16[1184,1024]{1,0:T(8,128)(2,1)} %bitcast.239, bf16[4096,1024]{1,0:T(8,128)(2,1)} %all-gather.13.cloned.1.call-done), kind=kOutput, calls=%fused_computation.7 | convolution fusion | flops 10000003072 | bytes 39927808 | tf_op jit(solution)/shard_map/dot_general | solution.py:25
  322.0 19.3 %convolution_convert_fusion = bf16[1024,4096]{1,0:T(8,128)(2,1)} fusion(bf16[1184,4096]{1,0:T(8,128)(2,1)} %get-tuple-element.63, f32[1184,1024]{1,0:T(8,128)} %fusion.7, f32[1024]{0:T(1024)S(1)} %reshape.256, f32[1024]{0:T(1024)S(1)} %reshape.255, f32[1184]{0:T(1024)S(1)} %add_rsqrt_fusion.1, f32[1184]{0:T(1024)S(1)} %broadcast_multiply_fusion.6), kind=kOutput, calls=%fused_computation.14 | convolution fusion | flops 9942368256 | bytes 22955264 | tf_op jit(solution)/shard_map/dot_general | solution.py:29
  341.3 19.5 %multiply_reduce_fusion = (f32[1024]{0:T(1024)S(1)}, f32[1184]{0:T(1024)S(1)}, f32[1184]{0:T(1024)S(1)}, f32[1024]{0:T(1024)S(1)}, f32[1184,1024]{1,0:T(8,128)}) fusion(f32[1184,1024]{1,0:T(8,128)} %fusion.7, f32[1184]{0:T(1024)S(1)} %add_rsqrt_fusion.1, f32[1184]{0:T(1024)S(1)} %broadcast_multiply_fusion.6, f32[1024]{0:T(1024)S(1)} %reshape.255, ...), kind=kOutput, calls=%fused_computation.21 | convolution fusion | flops 9943019520 | bytes 27818496 | tf_op jit(solution)/shard_map/dot_general | solution.py:25
  360.9 3.6 convert_reduce_fusion.3
  364.6 4.2 convolution_convert_fusion.4
  368.8 4.0 convolution_convert_fusion.3.g_ref
  372.8 50.4 %attend_back.1 = (bf16[1184,1024]{1,0:T(8,128)(2,1)S(1)}, bf16[1184,1024]{1,0:T(8,128)(2,1)S(1)}, bf16[1184,1024]{1,0:T(8,128)(2,1)}) custom-call(bf16[1184,3072]{1,0:T(8,128)(2,1)} %copy-done, bf16[1184,3072]{1,0:T(8,128)(2,1)} %copy-done, bf16[1184,3072]{1,0:T(8,128)(2,1)} %copy-done, bf16[1184,1024]{1,0:T(8,128)(2,1)} %convolution_convert_fusion.3.g_ref, ...), custom_call_target="tpu_custom_call" | custom-call | flops 28710010880 | bytes 16973824 | tf_op jit(solution)/shard_map/attend_back/pallas_call | solution.py:125
  426.2 3.5 slice-done.3
  429.7 10.5 %convolution_convert_fusion.2 = bf16[1024,3072]{1,0:T(8,128)(2,1)} fusion(bf16[1184,3072]{1,0:T(8,128)(2,1)S(1)} %constant_dynamic-update-slice_fusion, f32[1184,1024]{1,0:T(8,128)S(1)} %bitcast.243, f32[1024]{0:T(1024)S(1)} %copy-done.31, f32[1024]{0:T(1024)S(1)} %copy-done.27), kind=kOutput, calls=%fused_computation.16 | convolution fusion | flops 7455866880 | bytes 18423808 | tf_op jit(solution)/shard_map/dot_general | solution.py:29
  440.2 13.8 %convolution_convert_fusion.1 = bf16[4096,1024]{1,0:T(8,128)(2,1)S(1)} fusion(bf16[1184,4096]{1,0:T(8,128)(2,1)} %get-tuple-element.58, bf16[1184,1024]{1,0:T(8,128)(2,1)S(1)} %bitcast.240), kind=kOutput, calls=%fused_computation.15 | convolution fusion | flops 9936306176 | bytes 20512768 | tf_op jit(solution)/shard_map/dot_general | solution.py:29
  454.1 15.4 %add_convert_fusion.2 = bf16[1184,1024]{1,0:T(8,128)(2,1)S(1)} fusion(f32[1184,1024]{1,0:T(8,128)S(1)} %bitcast.226, bf16[1184,4096]{1,0:T(8,128)(2,1)} %get-tuple-element.58, bf16[4096,1024]{1,0:T(8,128)(2,1)} %all-gather.13.cloned.1.call-done, f32[1024]{0:T(1024)S(1)} %copy-done.29), kind=kOutput, calls=%fused_computation.28 | convolution fusion | flops 9935749120 | bytes 25366528 | tf_op jit(solution)/shard_map/dot_general | solution.py:21
  469.7 3.8 copy.52
  473.6 3.8 fusion.11
  479.2 6.8 fusion.12
  488.3 3.8 dynamic-slice_bitcast_fusion.2
  495.4 15.1 %multiply_reduce_fusion.1 = (f32[1024]{0:T(1024)S(1)}, f32[1184]{0:T(1024)S(1)}, f32[1184]{0:T(1024)S(1)}, f32[1024]{0:T(1024)S(1)}, f32[1184,1024]{1,0:T(8,128)}) fusion(f32[1184,1024]{1,0:T(8,128)} %fusion.6, f32[1024]{0:T(1024)S(1)} %copy-done.27, bf16[1184,3072]{1,0:T(8,128)(2,1)} %copy-done.10, bf16[1024,3072]{1,0:T(8,128)(2,1)} %all-gather.7.cloned.1.call-done), kind=kOutput, calls=%fused_computation.23 | convolution fusion | flops 7457566720 | bytes 23287040 | tf_op jit(solution)/shard_map/dot_general | solution.py:25
  510.6 4.9 fusion.13
  515.9 39.7 %all-reduce.2 = f32[32,384]{1,0:T(8,128)S(1)} all-reduce(f32[32,384]{1,0:T(8,128)S(1)} %concatenate.38), channel_id=3, replica_groups=mesh['dev'=8,'rep'=4] {'dev','rep'}, use_global_device_ids=true, to_apply=%region_16.17.clone | all-reduce | flops 12288 | bytes 98304
  557.1 6.4 add_convert_fusion.1
  566.5 3.8 copy.53
  573.2 2.3 collective-permute-start.11
  576.6 5.8 collective-permute-done.11
  582.4 1.8 collective-permute-start.16
  584.3 6.2 collective-permute-done.16
  592.2 3.3 collective-permute-done.12
  597.1 3.4 collective-permute-done.17
  601.4 6.1 collective-permute-done.13
  607.6 5.1 collective-permute-done.18
  612.7 3.9 collective-permute-done.14
  616.6 3.9 collective-permute-done.19
  626.2 2.1 bitcast_add_fusion.1
  631.1 11.4 %collective-permute-done.1 = bf16[2,2,2,32,1536]{4,3,2,1,0:T(8,128)(2,1)S(1)} collective-permute-done((bf16[2,2,2,32,1536]{4,3,2,1,0:T(8,128)(2,1)S(1)}, bf16[2,2,2,32,1536]{4,3,2,1,0:T(8,128)(2,1)S(1)}, u32[]{:S(2)}, u32[]{:S(2)}) %collective-permute-start.1) | collective-permute-done | bytes 786464 | tf_op jit(solution)/shard_map/ppermute | solution.py:173
  645.8 50.4 %collective-permute-done.2 = bf16[2,2,32,1536]{3,2,1,0:T(8,128)(2,1)S(1)} collective-permute-done((bf16[2,2,32,1536]{3,2,1,0:T(8,128)(2,1)S(1)}, bf16[2,2,32,1536]{3,2,1,0:T(8,128)(2,1)S(1)}, u32[]{:S(2)}, u32[]{:S(2)}) %collective-permute-start.2) | collective-permute-done | bytes 393248 | tf_op jit(solution)/shard_map/ppermute | solution.py:173
  697.1 9.1 %collective-permute-done.7 = bf16[2,2,32,1536]{3,2,1,0:T(8,128)(2,1)S(1)} collective-permute-done((bf16[2,2,32,1536]{3,2,1,0:T(8,128)(2,1)S(1)}, bf16[2,2,32,1536]{3,2,1,0:T(8,128)(2,1)S(1)}, u32[]{:S(2)}, u32[]{:S(2)}) %collective-permute-start.7) | collective-permute-done | bytes 393248 | tf_op jit(solution)/shard_map/ppermute | solution.py:173
  706.6 8.8 %collective-permute-done.3 = bf16[2,32,1536]{2,1,0:T(8,128)(2,1)S(1)} collective-permute-done((bf16[2,32,1536]{2,1,0:T(8,128)(2,1)S(1)}, bf16[2,32,1536]{2,1,0:T(8,128)(2,1)S(1)}, u32[]{:S(2)}, u32[]{:S(2)}) %collective-permute-start.3) | collective-permute-done | bytes 196640 | tf_op jit(solution)/shard_map/ppermute | solution.py:173
  715.5 10.1 %collective-permute-done.8 = bf16[2,32,1536]{2,1,0:T(8,128)(2,1)S(1)} collective-permute-done((bf16[2,32,1536]{2,1,0:T(8,128)(2,1)S(1)}, bf16[2,32,1536]{2,1,0:T(8,128)(2,1)S(1)}, u32[]{:S(2)}, u32[]{:S(2)}) %collective-permute-start.8) | collective-permute-done | bytes 196640 | tf_op jit(solution)/shard_map/ppermute | solution.py:173
  725.7 4.7 collective-permute-done.4
  730.6 4.3 collective-permute-done.9
  740.9 10.0 %collective-permute-done.32 = bf16[2,2,128,512]{3,2,1,0:T(8,128)(2,1)S(1)} collective-permute-done((bf16[2,2,128,512]{3,2,1,0:T(8,128)(2,1)S(1)}, bf16[2,2,128,512]{3,2,1,0:T(8,128)(2,1)S(1)}, u32[]{:S(2)}, u32[]{:S(2)}) %collective-permute-start.32) | collective-permute-done | bytes 524320 | tf_op jit(solution)/shard_map/ppermute | solution.py:173
  754.1 5.0 collective-permute-done.22
  762.3 15.5 %collective-permute-done.33 = bf16[2,128,512]{2,1,0:T(8,128)(2,1)S(1)} collective-permute-done((bf16[2,128,512]{2,1,0:T(8,128)(2,1)S(1)}, bf16[2,128,512]{2,1,0:T(8,128)(2,1)S(1)}, u32[]{:S(2)}, u32[]{:S(2)}) %collective-permute-start.33) | collective-permute-done | bytes 262176 | tf_op jit(solution)/shard_map/ppermute | solution.py:173
  778.0 5.6 collective-permute-done.38
  783.7 5.5 collective-permute-done.23
  789.3 4.3 collective-permute-done.28
  793.8 8.3 %collective-permute-done.24 = bf16[32,2048]{1,0:T(8,128)(2,1)S(1)} collective-permute-done((bf16[32,2048]{1,0:T(8,128)(2,1)S(1)}, bf16[32,2048]{1,0:T(8,128)(2,1)S(1)}, u32[]{:S(2)}, u32[]{:S(2)}) %collective-permute-start.24) | collective-permute-done | bytes 131104 | tf_op jit(solution)/shard_map/ppermute | solution.py:173
  (272 shorter events, 62.5 us)
Async XLA Ops:
  7.2 85.6 %copy-start.2 = (bf16[2,577,1024]{2,0,1:T(2,128)(2,1)S(1)}, bf16[2,577,1024]{2,0,1:T(2,128)(2,1)}, u32[]{:S(2)}) copy-start(bf16[2,577,1024]{2,0,1:T(2,128)(2,1)} %param.15) | copy-start | bytes 7090180
  7.2 115.4 %all-gather.7.cloned.1.call-start = ((), (), s32[]{:S(2)}) async-start(), calls=%async_computation | async-start | bytes 6488064 | tf_op jit(solution)/shard_map/all_gather | solution.py:218
  7.9 164.0 %all-gather.9.cloned.1.call-start = ((), (), s32[]{:S(2)}) async-start(), calls=%async_computation.1 | async-start | bytes 2162688 | tf_op jit(solution)/shard_map/all_gather | solution.py:218
  8.7 212.0 %all-gather.11.cloned.1.call-start = ((), (), s32[]{:S(2)}) async-start(), calls=%async_computation.2 | async-start | bytes 8650752 | tf_op jit(solution)/shard_map/all_gather | solution.py:218
  9.4 290.1 %all-gather.13.cloned.1.call-start = ((), (), s32[]{:S(2)}) async-start(), calls=%async_computation.3 | async-start | bytes 8650752 | tf_op jit(solution)/shard_map/all_gather | solution.py:218
  88.2 34.4 %copy-start.26 = (f32[1024]{0:T(1024)}, f32[1024]{0:T(1024)S(1)}, u32[]{:S(2)}) copy-start(f32[1024]{0:T(1024)S(1)} %reshape.252) | copy-start | bytes 12292
  88.3 34.3 %copy-start.30 = (f32[1024]{0:T(1024)}, f32[1024]{0:T(1024)S(1)}, u32[]{:S(2)}) copy-start(f32[1024]{0:T(1024)S(1)} %reshape.253) | copy-start | bytes 12292
  101.7 16.7 %copy-start.21 = (f32[1184]{0:T(1024)}, f32[1184]{0:T(1024)S(1)}, u32[]{:S(2)}) copy-start(f32[1184]{0:T(1024)S(1)} %rsqrt.20) | copy-start | bytes 14212
  101.8 16.6 %copy-start.23 = (f32[1184]{0:T(1024)}, f32[1184]{0:T(1024)S(1)}, u32[]{:S(2)}) copy-start(f32[1184]{0:T(1024)S(1)} %div.27) | copy-start | bytes 14212
  322.0 38.9 %slice-start = ((s8[4849664]{0:T(1024)(128)(4,1)}), s8[4194304]{0:T(1024)(128)(4,1)S(1)}, s32[]{:S(2)}) async-start(s8[4849664]{0:T(1024)(128)(4,1)} %bitcast.225), calls=%async_computation.4 | async-start | bytes 8388608
  341.3 19.5 %slice-start.1 = ((s8[4849664]{0:T(1024)(128)(4,1)}), s8[655360]{0:T(1024)(128)(4,1)S(1)}, s32[]{:S(2)}) async-start(s8[4849664]{0:T(1024)(128)(4,1)} %bitcast.225), calls=%async_computation.5 | async-start | bytes 1310720
  341.3 19.5 %copy-start.12 = (bf16[2,592,1024]{2,1,0:T(8,128)(2,1)S(1)}, bf16[2,592,1024]{2,1,0:T(8,128)(2,1)}, u32[]{:S(2)}) copy-start(bf16[2,592,1024]{2,1,0:T(8,128)(2,1)} %pad.8.clone) | copy-start | bytes 7274500
  425.1 15.1 %copy-start.10 = (bf16[1184,3072]{1,0:T(8,128)(2,1)}, bf16[1184,3072]{1,0:T(8,128)(2,1)S(1)}, u32[]{:S(2)}) copy-start(bf16[1184,3072]{1,0:T(8,128)(2,1)S(1)} %constant_dynamic-update-slice_fusion) | copy-start | bytes 21823492
  440.2 13.8 %copy-start.29 = (f32[1024]{0:T(1024)S(1)}, f32[1024]{0:T(1024)}, u32[]{:S(2)}) copy-start(f32[1024]{0:T(1024)} %reshape.258) | copy-start | bytes 12292
  479.2 6.9 copy-start.14
  479.2 7.8 copy-start.16
  487.0 6.6 copy-start.5
  487.8 83.6 %collective-permute-start.10 = (bf16[2,2,2,2,32,512]{5,4,3,2,1,0:T(8,128)(2,1)}, bf16[2,2,2,2,32,512]{5,4,3,2,1,0:T(8,128)(2,1)}, u32[]{:S(2)}, u32[]{:S(2)}) collective-permute-start(bf16[2,2,2,2,32,512]{5,4,3,2,1,0:T(8,128)(2,1)} %dynamic-slice_bitcast_fusion.17), channel_id=1, source_target_pairs={{0,4},{1,5},{2,6},{3,7},{4,0},{5,1},{6,2},{7,3},{8,12},{9,13},{10,... | collective-permute-start | bytes 1572872 | tf_op jit(solution)/shard_map/ppermute | solution.py:173
  488.1 85.1 %collective-permute-start.15 = (bf16[2,2,2,2,32,512]{5,4,3,2,1,0:T(8,128)(2,1)}, bf16[2,2,2,2,32,512]{5,4,3,2,1,0:T(8,128)(2,1)}, u32[]{:S(2)}, u32[]{:S(2)}) collective-permute-start(bf16[2,2,2,2,32,512]{5,4,3,2,1,0:T(8,128)(2,1)} %dynamic-slice_bitcast_fusion.16), channel_id=1, source_target_pairs={{0,4},{1,5},{2,6},{3,7},{4,0},{5,1},{6,2},{7,3},{8,12},{9,13},{10,... | collective-permute-start | bytes 1572872 | tf_op jit(solution)/shard_map/ppermute | solution.py:173
  495.1 130.4 %collective-permute-start.35 = (bf16[2,2,2,2,128,512]{5,4,3,2,1,0:T(8,128)(2,1)}, bf16[2,2,2,2,128,512]{5,4,3,2,1,0:T(8,128)(2,1)}, u32[]{:S(2)}, u32[]{:S(2)}) collective-permute-start(bf16[2,2,2,2,128,512]{5,4,3,2,1,0:T(8,128)(2,1)} %dynamic-slice_bitcast_fusion), channel_id=1, source_target_pairs={{0,4},{1,5},{2,6},{3,7},{4,0},{5,1},{6,2},{7,3},{8,12},{9,13},{10,... | collective-permute-start | bytes 6291464 | tf_op jit(solution)/shard_map/ppermute | solution.py:173
  510.6 46.5 %copy-start.22 = (f32[1184]{0:T(1024)S(1)}, f32[1184]{0:T(1024)}, u32[]{:S(2)}) copy-start(f32[1184]{0:T(1024)} %copy-done.21) | copy-start | bytes 14212
  510.6 46.5 %copy-start.24 = (f32[1184]{0:T(1024)S(1)}, f32[1184]{0:T(1024)}, u32[]{:S(2)}) copy-start(f32[1184]{0:T(1024)} %copy-done.23) | copy-start | bytes 14212
  557.1 7.0 copy-start.9
  564.3 59.4 %collective-permute-start.30 = (bf16[2,2,2,2,128,512]{5,4,3,2,1,0:T(8,128)(2,1)S(1)}, bf16[2,2,2,2,128,512]{5,4,3,2,1,0:T(8,128)(2,1)S(1)}, u32[]{:S(2)}, u32[]{:S(2)}) collective-permute-start(bf16[2,2,2,2,128,512]{5,4,3,2,1,0:T(8,128)(2,1)S(1)} %dynamic-slice_bitcast_fusion.1), channel_id=1, source_target_pairs={{0,4},{1,5},{2,6},{3,7},{4,0},{5,1},{6,2},{7,3},{8,12},{9,13},{10,... | collective-permute-start | bytes 6291464 | tf_op jit(solution)/shard_map/ppermute | solution.py:173
  566.2 9.2 %copy-start.15 = (bf16[1024,512]{1,0:T(8,128)(2,1)S(1)}, bf16[1024,512]{1,0:T(8,128)(2,1)}, u32[]{:S(2)}) copy-start(bf16[1024,512]{1,0:T(8,128)(2,1)} %copy-done.14) | copy-start | bytes 3145732
  570.3 50.2 %copy-start.20 = (bf16[2,2,2,2,32,2048]{5,4,3,2,1,0:T(8,128)(2,1)S(1)}, bf16[2,2,2,2,32,2048]{5,4,3,2,1,0:T(8,128)(2,1)}, u32[]{:S(2)}) copy-start(bf16[2,2,2,2,32,2048]{5,4,3,2,1,0:T(8,128)(2,1)} %dynamic-slice_bitcast_fusion.3) | copy-start | bytes 6291460
  570.3 50.9 %copy-start.19 = (bf16[2,2,2,2,32,2048]{5,4,3,2,1,0:T(8,128)(2,1)S(1)}, bf16[2,2,2,2,32,2048]{5,4,3,2,1,0:T(8,128)(2,1)}, u32[]{:S(2)}) copy-start(bf16[2,2,2,2,32,2048]{5,4,3,2,1,0:T(8,128)(2,1)} %dynamic-slice_bitcast_fusion.2) | copy-start | bytes 6291460
  570.3 51.4 %copy-start.11 = (bf16[1024,1536]{1,0:T(8,128)(2,1)S(1)}, bf16[1024,1536]{1,0:T(8,128)(2,1)}, u32[]{:S(2)}) copy-start(bf16[1024,1536]{1,0:T(8,128)(2,1)} %get-tuple-element.38) | copy-start | bytes 9437188
  570.3 50.9 %collective-permute-start = (bf16[2,2,2,2,32,1536]{5,4,3,2,1,0:T(8,128)(2,1)S(1)}, bf16[2,2,2,2,32,1536]{5,4,3,2,1,0:T(8,128)(2,1)S(1)}, u32[]{:S(2)}, u32[]{:S(2)}) collective-permute-start(bf16[2,2,2,2,32,1536]{5,4,3,2,1,0:T(8,128)(2,1)S(1)} %dynamic-slice_bitcast_fusion.5), channel_id=1, source_target_pairs={{0,4},{1,5},{2,6},{3,7},{4,0},{5,1},{6,2},{7,3},{8,12},{9,13},{10,... | collective-permute-start | bytes 4718600 | tf_op jit(solution)/shard_map/ppermute | solution.py:173
  571.4 50.6 %collective-permute-start.5 = (bf16[2,2,2,2,32,1536]{5,4,3,2,1,0:T(8,128)(2,1)}, bf16[2,2,2,2,32,1536]{5,4,3,2,1,0:T(8,128)(2,1)S(1)}, u32[]{:S(2)}, u32[]{:S(2)}) collective-permute-start(bf16[2,2,2,2,32,1536]{5,4,3,2,1,0:T(8,128)(2,1)} %dynamic-slice_bitcast_fusion.4), channel_id=1, source_target_pairs={{0,4},{1,5},{2,6},{3,7},{4,0},{5,1},{6,2},{7,3},{8,12},{9,13},{10,... | collective-permute-start | bytes 4718600 | tf_op jit(solution)/shard_map/ppermute | solution.py:173
  573.2 9.2 %collective-permute-start.11 = (bf16[2,2,2,32,512]{4,3,2,1,0:T(8,128)(2,1)S(1)}, bf16[2,2,2,32,512]{4,3,2,1,0:T(8,128)(2,1)S(1)}, u32[]{:S(2)}, u32[]{:S(2)}) collective-permute-start(bf16[2,2,2,32,512]{4,3,2,1,0:T(8,128)(2,1)S(1)} %dynamic-slice_bitcast_fusion.25), channel_id=1, source_target_pairs={{0,8},{1,9},{2,10},{3,11},{4,12},{5,13},{6,14},{7,15},{8,0},{9,1},... | collective-permute-start | bytes 786440 | tf_op jit(solution)/shard_map/ppermute | solution.py:173
  582.4 8.1 collective-permute-start.16
  590.5 5.0 collective-permute-start.12
  595.5 5.0 collective-permute-start.17
  600.5 7.1 collective-permute-start.13
  607.5 5.2 collective-permute-start.18
  612.7 3.9 collective-permute-start.14
  616.6 3.9 collective-permute-start.19
  620.5 7.9 collective-permute-start.20
  621.2 8.7 %collective-permute-start.25 = (bf16[2,2,2,2,32,2048]{5,4,3,2,1,0:T(8,128)(2,1)S(1)}, bf16[2,2,2,2,32,2048]{5,4,3,2,1,0:T(8,128)(2,1)S(1)}, u32[]{:S(2)}, u32[]{:S(2)}) collective-permute-start(bf16[2,2,2,2,32,2048]{5,4,3,2,1,0:T(8,128)(2,1)S(1)} %copy-done.19), channel_id=1, source_target_pairs={{0,4},{1,5},{2,6},{3,7},{4,0},{5,1},{6,2},{7,3},{8,12},{9,13},{10,... | collective-permute-start | bytes 6291464 | tf_op jit(solution)/shard_map/ppermute | solution.py:173
  622.0 20.5 %collective-permute-start.1 = (bf16[2,2,2,32,1536]{4,3,2,1,0:T(8,128)(2,1)S(1)}, bf16[2,2,2,32,1536]{4,3,2,1,0:T(8,128)(2,1)S(1)}, u32[]{:S(2)}, u32[]{:S(2)}) collective-permute-start(bf16[2,2,2,32,1536]{4,3,2,1,0:T(8,128)(2,1)S(1)} %dynamic-slice_bitcast_fusion.11), channel_id=1, source_target_pairs={{0,8},{1,9},{2,10},{3,11},{4,12},{5,13},{6,14},{7,15},{8,0},{9,1},... | collective-permute-start | bytes 2359304 | tf_op jit(solution)/shard_map/ppermute | solution.py:173
  623.7 20.5 %collective-permute-start.6 = (bf16[2,2,2,32,1536]{4,3,2,1,0:T(8,128)(2,1)S(1)}, bf16[2,2,2,32,1536]{4,3,2,1,0:T(8,128)(2,1)S(1)}, u32[]{:S(2)}, u32[]{:S(2)}) collective-permute-start(bf16[2,2,2,32,1536]{4,3,2,1,0:T(8,128)(2,1)S(1)} %dynamic-slice_bitcast_fusion.10), channel_id=1, source_target_pairs={{0,16},{1,17},{2,18},{3,19},{4,20},{5,21},{6,22},{7,23},{8,24},{9,... | collective-permute-start | bytes 2359304 | tf_op jit(solution)/shard_map/ppermute | solution.py:173
  625.6 110.1 %collective-permute-start.31 = (bf16[2,2,2,128,512]{4,3,2,1,0:T(8,128)(2,1)S(1)}, bf16[2,2,2,128,512]{4,3,2,1,0:T(8,128)(2,1)S(1)}, u32[]{:S(2)}, u32[]{:S(2)}) collective-permute-start(bf16[2,2,2,128,512]{4,3,2,1,0:T(8,128)(2,1)S(1)} %dynamic-slice_bitcast_fusion.7), channel_id=1, source_target_pairs={{0,8},{1,9},{2,10},{3,11},{4,12},{5,13},{6,14},{7,15},{8,0},{9,1},... | collective-permute-start | bytes 3145736 | tf_op jit(solution)/shard_map/ppermute | solution.py:173
  628.4 109.1 %collective-permute-start.36 = (bf16[2,2,2,128,512]{4,3,2,1,0:T(8,128)(2,1)S(1)}, bf16[2,2,2,128,512]{4,3,2,1,0:T(8,128)(2,1)S(1)}, u32[]{:S(2)}, u32[]{:S(2)}) collective-permute-start(bf16[2,2,2,128,512]{4,3,2,1,0:T(8,128)(2,1)S(1)} %dynamic-slice_bitcast_fusion.6), channel_id=1, source_target_pairs={{0,16},{1,17},{2,18},{3,19},{4,20},{5,21},{6,22},{7,23},{8,24},{9,... | collective-permute-start | bytes 3145736 | tf_op jit(solution)/shard_map/ppermute | solution.py:173
  630.0 108.4 %collective-permute-start.21 = (bf16[2,2,2,32,2048]{4,3,2,1,0:T(8,128)(2,1)S(1)}, bf16[2,2,2,32,2048]{4,3,2,1,0:T(8,128)(2,1)S(1)}, u32[]{:S(2)}, u32[]{:S(2)}) collective-permute-start(bf16[2,2,2,32,2048]{4,3,2,1,0:T(8,128)(2,1)S(1)} %dynamic-slice_bitcast_fusion.9), channel_id=1, source_target_pairs={{0,8},{1,9},{2,10},{3,11},{4,12},{5,13},{6,14},{7,15},{8,0},{9,1},... | collective-permute-start | bytes 3145736 | tf_op jit(solution)/shard_map/ppermute | solution.py:173
  642.4 96.8 %collective-permute-start.26 = (bf16[2,2,2,32,2048]{4,3,2,1,0:T(8,128)(2,1)S(1)}, bf16[2,2,2,32,2048]{4,3,2,1,0:T(8,128)(2,1)S(1)}, u32[]{:S(2)}, u32[]{:S(2)}) collective-permute-start(bf16[2,2,2,32,2048]{4,3,2,1,0:T(8,128)(2,1)S(1)} %dynamic-slice_bitcast_fusion.8), channel_id=1, source_target_pairs={{0,16},{1,17},{2,18},{3,19},{4,20},{5,21},{6,22},{7,23},{8,24},{9,... | collective-permute-start | bytes 3145736 | tf_op jit(solution)/shard_map/ppermute | solution.py:173
  644.2 52.1 %collective-permute-start.2 = (bf16[2,2,32,1536]{3,2,1,0:T(8,128)(2,1)S(1)}, bf16[2,2,32,1536]{3,2,1,0:T(8,128)(2,1)S(1)}, u32[]{:S(2)}, u32[]{:S(2)}) collective-permute-start(bf16[2,2,32,1536]{3,2,1,0:T(8,128)(2,1)S(1)} %dynamic-slice_bitcast_fusion.19), channel_id=1, source_target_pairs={{0,16},{1,17},{2,18},{3,19},{4,20},{5,21},{6,22},{7,23},{8,24},{9,... | collective-permute-start | bytes 1179656 | tf_op jit(solution)/shard_map/ppermute | solution.py:173
  696.3 9.9 %collective-permute-start.7 = (bf16[2,2,32,1536]{3,2,1,0:T(8,128)(2,1)S(1)}, bf16[2,2,32,1536]{3,2,1,0:T(8,128)(2,1)S(1)}, u32[]{:S(2)}, u32[]{:S(2)}) collective-permute-start(bf16[2,2,32,1536]{3,2,1,0:T(8,128)(2,1)S(1)} %dynamic-slice_bitcast_fusion.18), channel_id=1, source_target_pairs={{0,8},{1,9},{2,10},{3,11},{4,12},{5,13},{6,14},{7,15},{8,0},{9,1},... | collective-permute-start | bytes 1179656 | tf_op jit(solution)/shard_map/ppermute | solution.py:173
  706.2 9.3 %collective-permute-start.3 = (bf16[2,32,1536]{2,1,0:T(8,128)(2,1)S(1)}, bf16[2,32,1536]{2,1,0:T(8,128)(2,1)S(1)}, u32[]{:S(2)}, u32[]{:S(2)}) collective-permute-start(bf16[2,32,1536]{2,1,0:T(8,128)(2,1)S(1)} %dynamic-slice_bitcast_fusion.27), channel_id=1, source_target_pairs={{0,2},{1,3},{2,0},{3,1},{4,6},{5,7},{6,4},{7,5},{8,10},{9,11},{10,... | collective-permute-start | bytes 589832 | tf_op jit(solution)/shard_map/ppermute | solution.py:173
  715.5 10.1 %collective-permute-start.8 = (bf16[2,32,1536]{2,1,0:T(8,128)(2,1)S(1)}, bf16[2,32,1536]{2,1,0:T(8,128)(2,1)S(1)}, u32[]{:S(2)}, u32[]{:S(2)}) collective-permute-start(bf16[2,32,1536]{2,1,0:T(8,128)(2,1)S(1)} %dynamic-slice_bitcast_fusion.26), channel_id=1, source_target_pairs={{0,2},{1,3},{2,0},{3,1},{4,6},{5,7},{6,4},{7,5},{8,10},{9,11},{10,... | collective-permute-start | bytes 589832 | tf_op jit(solution)/shard_map/ppermute | solution.py:173
  725.6 4.7 collective-permute-start.4
  730.3 4.6 collective-permute-start.9
  735.9 14.9 %collective-permute-start.32 = (bf16[2,2,128,512]{3,2,1,0:T(8,128)(2,1)S(1)}, bf16[2,2,128,512]{3,2,1,0:T(8,128)(2,1)S(1)}, u32[]{:S(2)}, u32[]{:S(2)}) collective-permute-start(bf16[2,2,128,512]{3,2,1,0:T(8,128)(2,1)S(1)} %dynamic-slice_bitcast_fusion.13), channel_id=1, source_target_pairs={{0,16},{1,17},{2,18},{3,19},{4,20},{5,21},{6,22},{7,23},{8,24},{9,... | collective-permute-start | bytes 1572872 | tf_op jit(solution)/shard_map/ppermute | solution.py:173
  737.7 14.9 %collective-permute-start.37 = (bf16[2,2,128,512]{3,2,1,0:T(8,128)(2,1)S(1)}, bf16[2,2,128,512]{3,2,1,0:T(8,128)(2,1)S(1)}, u32[]{:S(2)}, u32[]{:S(2)}) collective-permute-start(bf16[2,2,128,512]{3,2,1,0:T(8,128)(2,1)S(1)} %dynamic-slice_bitcast_fusion.12), channel_id=1, source_target_pairs={{0,8},{1,9},{2,10},{3,11},{4,12},{5,13},{6,14},{7,15},{8,0},{9,1},... | collective-permute-start | bytes 1572872 | tf_op jit(solution)/shard_map/ppermute | solution.py:173
  738.6 20.5 %collective-permute-start.22 = (bf16[2,2,32,2048]{3,2,1,0:T(8,128)(2,1)S(1)}, bf16[2,2,32,2048]{3,2,1,0:T(8,128)(2,1)S(1)}, u32[]{:S(2)}, u32[]{:S(2)}) collective-permute-start(bf16[2,2,32,2048]{3,2,1,0:T(8,128)(2,1)S(1)} %dynamic-slice_bitcast_fusion.15), channel_id=1, source_target_pairs={{0,16},{1,17},{2,18},{3,19},{4,20},{5,21},{6,22},{7,23},{8,24},{9,... | collective-permute-start | bytes 1572872 | tf_op jit(solution)/shard_map/ppermute | solution.py:173
  739.5 21.1 %collective-permute-start.27 = (bf16[2,2,32,2048]{3,2,1,0:T(8,128)(2,1)S(1)}, bf16[2,2,32,2048]{3,2,1,0:T(8,128)(2,1)S(1)}, u32[]{:S(2)}, u32[]{:S(2)}) collective-permute-start(bf16[2,2,32,2048]{3,2,1,0:T(8,128)(2,1)S(1)} %dynamic-slice_bitcast_fusion.14), channel_id=1, source_target_pairs={{0,8},{1,9},{2,10},{3,11},{4,12},{5,13},{6,14},{7,15},{8,0},{9,1},... | collective-permute-start | bytes 1572872 | tf_op jit(solution)/shard_map/ppermute | solution.py:173
  751.0 26.9 %collective-permute-start.33 = (bf16[2,128,512]{2,1,0:T(8,128)(2,1)S(1)}, bf16[2,128,512]{2,1,0:T(8,128)(2,1)S(1)}, u32[]{:S(2)}, u32[]{:S(2)}) collective-permute-start(bf16[2,128,512]{2,1,0:T(8,128)(2,1)S(1)} %dynamic-slice_bitcast_fusion.21), channel_id=1, source_target_pairs={{0,2},{1,3},{2,0},{3,1},{4,6},{5,7},{6,4},{7,5},{8,10},{9,11},{10,... | collective-permute-start | bytes 786440 | tf_op jit(solution)/shard_map/ppermute | solution.py:173
  752.8 30.8 %collective-permute-start.38 = (bf16[2,128,512]{2,1,0:T(8,128)(2,1)S(1)}, bf16[2,128,512]{2,1,0:T(8,128)(2,1)S(1)}, u32[]{:S(2)}, u32[]{:S(2)}) collective-permute-start(bf16[2,128,512]{2,1,0:T(8,128)(2,1)S(1)} %dynamic-slice_bitcast_fusion.20), channel_id=1, source_target_pairs={{0,2},{1,3},{2,0},{3,1},{4,6},{5,7},{6,4},{7,5},{8,10},{9,11},{10,... | collective-permute-start | bytes 786440 | tf_op jit(solution)/shard_map/ppermute | solution.py:173
  759.2 30.0 %collective-permute-start.23 = (bf16[2,32,2048]{2,1,0:T(8,128)(2,1)S(1)}, bf16[2,32,2048]{2,1,0:T(8,128)(2,1)S(1)}, u32[]{:S(2)}, u32[]{:S(2)}) collective-permute-start(bf16[2,32,2048]{2,1,0:T(8,128)(2,1)S(1)} %dynamic-slice_bitcast_fusion.23), channel_id=1, source_target_pairs={{0,2},{1,3},{2,0},{3,1},{4,6},{5,7},{6,4},{7,5},{8,10},{9,11},{10,... | collective-permute-start | bytes 786440 | tf_op jit(solution)/shard_map/ppermute | solution.py:173
  760.7 32.9 %collective-permute-start.28 = (bf16[2,32,2048]{2,1,0:T(8,128)(2,1)S(1)}, bf16[2,32,2048]{2,1,0:T(8,128)(2,1)S(1)}, u32[]{:S(2)}, u32[]{:S(2)}) collective-permute-start(bf16[2,32,2048]{2,1,0:T(8,128)(2,1)S(1)} %dynamic-slice_bitcast_fusion.22), channel_id=1, source_target_pairs={{0,2},{1,3},{2,0},{3,1},{4,6},{5,7},{6,4},{7,5},{8,10},{9,11},{10,... | collective-permute-start | bytes 786440 | tf_op jit(solution)/shard_map/ppermute | solution.py:173
  777.9 24.2 %collective-permute-start.34 = (bf16[128,512]{1,0:T(8,128)(2,1)S(1)}, bf16[128,512]{1,0:T(8,128)(2,1)S(1)}, u32[]{:S(2)}, u32[]{:S(2)}) collective-permute-start(bf16[128,512]{1,0:T(8,128)(2,1)S(1)} %dynamic-slice_bitcast_fusion.29), channel_id=1, source_target_pairs={{0,1},{1,0},{2,3},{3,2},{4,5},{5,4},{6,7},{7,6},{8,9},{9,8},{10,11... | collective-permute-start | bytes 393224 | tf_op jit(solution)/shard_map/ppermute | solution.py:173
  783.6 18.5 %collective-permute-start.39 = (bf16[128,512]{1,0:T(8,128)(2,1)S(1)}, bf16[128,512]{1,0:T(8,128)(2,1)S(1)}, u32[]{:S(2)}, u32[]{:S(2)}) collective-permute-start(bf16[128,512]{1,0:T(8,128)(2,1)S(1)} %dynamic-slice_bitcast_fusion.28), channel_id=1, source_target_pairs={{0,1},{1,0},{2,3},{3,2},{4,5},{5,4},{6,7},{7,6},{8,9},{9,8},{10,11... | collective-permute-start | bytes 393224 | tf_op jit(solution)/shard_map/ppermute | solution.py:173
  789.2 12.8 %collective-permute-start.24 = (bf16[32,2048]{1,0:T(8,128)(2,1)S(1)}, bf16[32,2048]{1,0:T(8,128)(2,1)S(1)}, u32[]{:S(2)}, u32[]{:S(2)}) collective-permute-start(bf16[32,2048]{1,0:T(8,128)(2,1)S(1)} %dynamic-slice_bitcast_fusion.31), channel_id=1, source_target_pairs={{0,1},{1,0},{2,3},{3,2},{4,5},{5,4},{6,7},{7,6},{8,9},{9,8},{10,11... | collective-permute-start | bytes 393224 | tf_op jit(solution)/shard_map/ppermute | solution.py:173
  793.7 11.1 %collective-permute-start.29 = (bf16[32,2048]{1,0:T(8,128)(2,1)S(1)}, bf16[32,2048]{1,0:T(8,128)(2,1)S(1)}, u32[]{:S(2)}, u32[]{:S(2)}) collective-permute-start(bf16[32,2048]{1,0:T(8,128)(2,1)S(1)} %dynamic-slice_bitcast_fusion.30), channel_id=1, source_target_pairs={{0,1},{1,0},{2,3},{3,2},{4,5},{5,4},{6,7},{7,6},{8,9},{9,8},{10,11... | collective-permute-start | bytes 393224 | tf_op jit(solution)/shard_map/ppermute | solution.py:173
  (17 other events, 67.3 us)
Sparse Core Ops, SparseCore 0:
  10.9 72.5 all-gather.6
  86.4 55.0 all-gather.8
  144.4 76.2 all-gather.10
  223.5 75.9 all-gather.12

commit v2 on v1

--- a/solution.py
+++ b/solution.py
@@ -1,4 +1,5 @@
 import functools
+import heapq
 import math
 
 import jax
@@ -10,6 +11,11 @@
 
 HEADS = 16
 HD = 64
+MESH = pl.DeviceIdType.MESH
+FAST_MESH = (8, 4)
+GRID_STEPS = 16
+STEP_US = {"attend": 2.2}
+DEPTH = 4
 LANES = 128
 EPS = 1e-06
 AXES = ("dev", "rep")
@@ -34,11 +40,10 @@
     return [(lane >= h * HD) & (lane < (h + 1) * HD) for h in range(LANES // HD)]
 
 
-def attend_kernel(seq, scale, q_ref, k_ref, v_ref, out_ref, log_ref):
+def attend_pair(seq, scale, q_ref, k_ref, v_ref, out_ref, log_ref):
     queries = q_ref[...]
     keys = k_ref[...] * jnp.asarray(scale, BF)
     values = v_ref[...]
-    rows = queries.shape[0]
     masks = head_masks(queries.shape)
     zero = jnp.zeros((), BF)
     total = None
@@ -54,6 +59,49 @@
         total = mixed if total is None else total + mixed
         log_ref[0, 0, h : h + 1, :] = highest + jnp.log(sums)
     out_ref[...] = total.astype(BF)
+
+
+def attend_kernel(seq, scale, count, q_ref, k_ref, v_ref, *refs):
+    shards, (out_ref, log_ref), fulls = refs[:count], refs[count : count + 2], refs[count + 2 : 2 * count + 2]
+    compute = functools.partial(attend_pair, seq, scale, q_ref, k_ref, v_ref, out_ref, log_ref)
+    if count == 0:
+        compute()
+        return
+    send_sems, recv_sems, own_sems = refs[2 * count + 2 :]
+    at = place()
+    copies = Copies(at, send_sems, recv_sems)
+    owns, steps = gather_plan(copies, shards, fulls, own_sems)
+
+    def begin():
+        greet(at)
+        for own in owns:
+            own().start()
+
+    beside(compute, STEP_US["attend"], steps, begin, copies.drain)
+
+
+def beside(compute, step_us, steps, first, last):
+    now = pl.program_id(0) * pl.num_programs(1) + pl.program_id(1)
+    ends = GRID_STEPS - 1
+    groups = [[] for _ in range(GRID_STEPS)]
+    for ready, run in steps:
+        groups[min(ends, int(ready / step_us))].append(run)
+    pl.when(now == 0)(first)
+    for number, group in enumerate(groups[:-1]):
+        if group:
+
+            @pl.when(now == number)
+            def _(group=group):
+                for run in group:
+                    run()
+
+    compute()
+
+    @pl.when(now == ends)
+    def _():
+        for run in groups[-1]:
+            run()
+        last()
 
 
 def attend_back_kernel(seq, scale, q_ref, k_ref, v_ref, g_ref, log_ref, dq_ref, dk_ref, dv_ref):
@@ -83,34 +131,42 @@
     dv_ref[...] = dv.astype(BF)
 
 
-def attend(joined, images_now, rows, seq, scale):
+def attend(joined, images_now, rows, seq, scale, shards=()):
     width = joined.shape[1] // 3
     pairs = width // LANES
+    heads = LANES // HD
+    count = len(shards)
+    anywhere = pl.BlockSpec(memory_space=pl.ANY)
 
     def part(which):
         return pl.BlockSpec((rows, LANES), lambda i, j: (i, which * pairs + j))
 
-    heads = LANES // HD
+    params = dict(vmem_limit_bytes=40 << 20)
+    if count:
+        params.update(collective_id=1, has_side_effects=True)
     return pl.pallas_call(
-        functools.partial(attend_kernel, seq, scale),
+        functools.partial(attend_kernel, seq, scale, count),
         grid=(images_now, pairs),
-        in_specs=[part(0), part(1), part(2)],
+        in_specs=[part(0), part(1), part(2)] + [anywhere] * count,
         out_specs=[
             pl.BlockSpec((rows, LANES), lambda i, j: (i, j)),
             pl.BlockSpec((1, 1, heads, rows), lambda i, j: (i, j, 0, 0)),
-        ],
+        ]
+        + [anywhere] * count,
         out_shape=[
             jax.ShapeDtypeStruct((images_now * rows, width), BF),
             jax.ShapeDtypeStruct((images_now, pairs, heads, rows), F32),
-        ],
-        compiler_params=pltpu.CompilerParams(vmem_limit_bytes=40 << 20),
+        ]
+        + gathered_shapes(shards),
+        scratch_shapes=gather_scratch(shards) if count else [],
+        compiler_params=pltpu.CompilerParams(**params),
         cost_estimate=pl.CostEstimate(
             flops=4 * images_now * HEADS * rows * rows * LANES * 2,
             bytes_accessed=images_now * rows * width * 8,
             transcendentals=images_now * HEADS * rows * rows,
         ),
         name="attend",
-    )(joined, joined, joined)
+    )(joined, joined, joined, *shards)
 
 
 def attend_back(joined, grads, logs, images_now, rows, seq, scale):
@@ -144,6 +200,266 @@
     )(joined, joined, joined, grads, logs)
 
 
+ORDERS = (("x", "z", "y"), ("y", "z", "x"), ("z", "x", "y"), ("z", "y", "x"))
+SHARES = (8, 8, 4, 4)
+
+
+def place():
+    dev = lax.axis_index("dev")
+    return dict(
+        core=dev % 2, x=(dev // 2) % 2, y=dev // 4, z=lax.axis_index("rep")
+    )
+
+
+def peer(at, axis, step=0):
+    other = dict(at)
+    other[axis] = at[axis] + step if axis == "z" else 1 - at[axis]
+    return {"dev": (other["y"] * 2 + other["x"]) * 2 + other["core"], "rep": other["z"]}
+
+
+def greet(at):
+    barrier = pltpu.get_barrier_semaphore()
+    for axis in ("core", "x", "y"):
+        pl.semaphore_signal(barrier, 1, device_id=peer(at, axis), device_id_type=MESH)
+    for step in (1, -1):
+
+        @pl.when((at["z"] + step >= 0) & (at["z"] + step < DEPTH))
+        def _():
+            pl.semaphore_signal(barrier, 1, device_id=peer(at, "z", step), device_id_type=MESH)
+
+    ends = (at["z"] == 0) | (at["z"] == DEPTH - 1)
+
+    @pl.when(ends)
+    def _():
+        pl.semaphore_wait(barrier, 4)
+
+    @pl.when(jnp.logical_not(ends))
+    def _():
+        pl.semaphore_wait(barrier, 5)
+
+
+def cuts(columns):
+    units = columns // 128
+    total = sum(SHARES)
+    out, at, seen = [], 0, 0
+    for order, share in zip(ORDERS, SHARES):
+        seen += share
+        end = round(units * seen / total)
+        if end > at:
+            out.append((order, at * 128, (end - at) * 128))
+        at = end
+    return out
+
+
+class Copy:
+    def __init__(self, owner, number, source, target, axis, step, sends, comes):
+        self.owner, self.number, self.source, self.target = owner, number, source, target
+        self.axis, self.step, self.sends, self.comes = axis, step, sends, comes
+
+    def build(self):
+        return pltpu.make_async_remote_copy(
+            src_ref=self.source(),
+            dst_ref=self.target(),
+            send_sem=self.owner.send_sems.at[self.number],
+            recv_sem=self.owner.recv_sems.at[self.number],
+            device_id=peer(self.owner.at, self.axis, self.step),
+            device_id_type=MESH,
+        )
+
+    def guarded(self, condition, act):
+        if condition is None:
+            act()
+        else:
+            pl.when(condition())(act)
+
+    def start(self):
+        self.guarded(self.sends, lambda: self.build().start())
+
+    def wait_send(self):
+        self.guarded(self.sends, lambda: self.build().wait_send())
+
+    def wait_recv(self):
+        self.guarded(self.comes, lambda: self.build().wait_recv())
+
+
+class Copies:
+    def __init__(self, at, send_sems, recv_sems):
+        self.at, self.send_sems, self.recv_sems = at, send_sems, recv_sems
+        self.all = []
+
+    def make(self, source, target, axis, step=0, sends=None, comes=None):
+        copy = Copy(self, len(self.all), source, target, axis, step, sends, comes)
+        self.all.append(copy)
+        return copy
+
+    def drain(self):
+        for copy in self.all:
+            copy.wait_send()
+
+
+LINK = {"x": 90.0, "y": 90.0, "zr": 90.0, "zl": 90.0, "core": 600.0}
+
+
+def issue_order(chains):
+    free = dict.fromkeys(LINK, 0.0)
+    queue = [(0.0, number, 0) for number in range(len(chains))]
+    heapq.heapify(queue)
+    out = []
+    while queue:
+        ready, number, step = heapq.heappop(queue)
+        links, size, run = chains[number][step]
+        out.append((ready, run))
+        done = ready
+        for link in links:
+            begin = max(free[link], ready)
+            free[link] = begin + size / LINK[link]
+            done = max(done, free[link] + 2.0)
+        if step + 1 < len(chains[number]):
+            heapq.heappush(queue, (done, number, step + 1))
+    return out
+
+
+def on_line(at, direction, hop):
+    def sends():
+        source, target = at["z"] - direction * (hop - 1), at["z"] + direction
+        return (source >= 0) & (source < DEPTH) & (target >= 0) & (target < DEPTH)
+
+    def comes():
+        source = at["z"] - direction * hop
+        return (source >= 0) & (source < DEPTH)
+
+    return sends, comes
+
+
+def gather_chain(copies, shard, full, order, columns, own_ready):
+    at = copies.at
+    steps = []
+    begin, width = columns
+    size = 2 * full.shape[4] * width * 2 / 1000.0
+    pending = []
+
+    def region(held, block_z=None):
+        def along(axis, extent):
+            return pl.ds(0, extent) if axis in held else at[axis]
+
+        z = pl.ds(0, DEPTH) if "z" in held else (at["z"] if block_z is None else block_z)
+        y, x = along("y", full.shape[0]), along("x", full.shape[1])
+        return full.at[y, x, at["core"], z, :, pl.ds(begin, width)]
+
+    def step(links, size, copies_now, own=False):
+        before = list(pending)
+        pending.clear()
+        pending.extend(copies_now)
+
+        def run():
+            if own:
+                own_ready()
+            for copy in before:
+                copy.wait_recv()
+            for copy in copies_now:
+                copy.start()
+
+        steps.append((links, size, run))
+
+    def first():
+        return shard.at[:, pl.ds(begin, width)]
+
+    held, blocks = (), 1
+    for axis in order:
+        here = functools.partial(region, held)
+        if axis == "z":
+            for hop in range(1, DEPTH):
+                now = []
+                for direction in (1, -1):
+
+                    def place_of(direction=direction, hop=hop, here=here):
+                        return here(at["z"] - direction * (hop - 1))
+
+                    source = first if blocks == 1 and hop == 1 else place_of
+                    sends, comes = on_line(at, direction, hop)
+                    now.append(copies.make(source, place_of, "z", direction, sends, comes))
+                step(("zr", "zl"), size * blocks, now, blocks > 1 and hop == 1)
+            blocks *= DEPTH
+        else:
+            copy = copies.make(first if blocks == 1 else here, here, axis)
+            step((axis,), size * blocks, [copy], blocks > 1)
+            blocks *= 2
+        held += (axis,)
+    whole = functools.partial(region, held)
+    step(("core",), size * blocks / 2, [copies.make(whole, whole, "core")])
+    step((), 0.0, [])
+    return steps
+
+
+def gather_plan(copies, shards, fulls, own_sems):
+    at = copies.at
+    chains, owns = [], []
+    for number, (shard, full) in enumerate(zip(shards, fulls)):
+
+        def own(number=number, shard=shard, full=full):
+            mine = full.at[at["y"], at["x"], at["core"], at["z"]]
+            return pltpu.make_async_copy(shard, mine, own_sems.at[number])
+
+        owns.append(own)
+        waited = []
+
+        def ready(own=own, waited=waited):
+            if not waited:
+                own().wait()
+                waited.append(True)
+
+        if full.shape[4] > 1:
+            parts = cuts(full.shape[5])
+        else:
+            parts = [(ORDERS[0], 0, full.shape[5])]
+        for order, begin, width in parts:
+            chains.append(gather_chain(copies, shard, full, order, (begin, width), ready))
+    return owns, issue_order(chains)
+
+
+def gathered_shapes(shards):
+    return [jax.ShapeDtypeStruct((2, 2, 2, DEPTH) + s.shape, s.dtype) for s in shards]
+
+
+def gather_scratch(shards):
+    count = 9 * sum(len(cuts(s.shape[1])) if s.shape[0] > 1 else 1 for s in shards)
+    return [
+        pltpu.SemaphoreType.DMA((count,)),
+        pltpu.SemaphoreType.DMA((count,)),
+        pltpu.SemaphoreType.DMA((len(shards),)),
+    ]
+
+
+def gather_kernel(count, *refs):
+    shards, fulls = refs[:count], refs[count : 2 * count]
+    send_sems, recv_sems, own_sems = refs[2 * count :]
+    at = place()
+    greet(at)
+    copies = Copies(at, send_sems, recv_sems)
+    owns, steps = gather_plan(copies, shards, fulls, own_sems)
+    for own in owns:
+        own().start()
+    for _, run in steps:
+        run()
+    copies.drain()
+
+
+def gather(shards, number):
+    count = len(shards)
+    anywhere = pl.BlockSpec(memory_space=pl.ANY)
+    return pl.pallas_call(
+        functools.partial(gather_kernel, count),
+        in_specs=[anywhere] * count,
+        out_specs=[anywhere] * count,
+        out_shape=gathered_shapes(shards),
+        scratch_shapes=gather_scratch(shards),
+        compiler_params=pltpu.CompilerParams(
+            collective_id=number, has_side_effects=True, vmem_limit_bytes=16 << 20
+        ),
+        name="gather_weights",
+    )(*shards)
+
+
 def index_bits(sizes):
     dev, rep = sizes
     out = []
@@ -208,14 +524,23 @@
     tokens = images_now * rows
     scale = 1.0 / math.sqrt(HD)
 
-    packed = lax.all_gather(jnp.concatenate(small_in), AXES, axis=0, tiled=False)
+    fast = sizes == FAST_MESH
+    joint_shard, proj_shard, up_shard, down_shard = big_in
+    packed = jnp.concatenate(small_in)[None]
+    if fast:
+        packed, joint_w = gather((packed, joint_shard), 0)
+        joint_w = joint_w.reshape(count * joint_shard.shape[0], -1)
+        later = (proj_shard, up_shard, down_shard)
+    else:
+        packed = lax.all_gather(packed, AXES, axis=0, tiled=False)
+        joint_w, proj_w, up_w, down_w = [lax.all_gather(w, AXES, axis=0, tiled=True) for w in big_in]
+        later = ()
     packed = packed.reshape(count, -1)
     smalls, at = [], 0
     for one in small_in:
         smalls.append(packed[:, at : at + one.shape[0]].reshape(-1).astype(F32))
         at += one.shape[0]
     gain_one, bias_one, joint_bias, proj_bias, gain_two, bias_two, up_bias, down_bias = smalls
-    joint_w, proj_w, up_w, down_w = [lax.all_gather(w, AXES, axis=0, tiled=True) for w in big_in]
 
     pad = ((0, 0), (0, rows - seq), (0, 0))
     residual_in = jnp.pad(images, pad).reshape(tokens, width).astype(F32)
@@ -223,7 +548,11 @@
     normed_one = (n_one * gain_one + bias_one).astype(BF)
     bias_full = jnp.concatenate([joint_bias[:width], jnp.zeros((width,), F32), joint_bias[width:]])
     joined = (mm(normed_one, joint_w) + bias_full).astype(BF)
-    heads_out, logs = attend(joined, images_now, rows, seq, scale)
+    heads_out, logs, *found = attend(joined, images_now, rows, seq, scale, later)
+    if fast:
+        proj_w, up_w, down_w = [
+            full.reshape(count * shard.shape[0], -1) for full, shard in zip(found, later)
+        ]
     middle = residual_in + mm(heads_out, proj_w) + proj_bias
     n_two, r_two = norm_stats(middle)
     normed_two = (n_two * gain_two + bias_two).astype(BF)

time: 816 us -> 747 us (0.915)
  Pallas kernels: 85.4 us -> 207 us
  waiting for transfers between devices: 292 us -> 194 us
  blocking collectives: 111 us -> 39.7 us
  other arithmetic: 52.3 us -> 37.4 us
  between operations: 15 us -> 2.32 us
    pallas_call x1 -> x2, Pallas kernels: 35 us -> 157 us  [the longest x1 112 us: attend(): pl.pallas_call(functools.partial(attend_kernel, seq, scale, count), grid=...]
    all_gather x4 -> x0, waiting for transfers between devices: 95.3 us -> none  [body(): lax.all_gather(w, AXES, axis=0, tiled=True)]
    all_gather x1 -> x0, blocking collectives: 70.9 us -> none  [body(): lax.all_gather(jnp.concatenate(small_in), AXES, axis=0, tiled=False)]
    unnamed x83 -> x116, local copies, waits for them, and re-layouts: 19.7 us -> 26.1 us
  transfers between devices with their start and end apart: 44 -> 40, of which waited for: 28 -> 28; matrix products, arithmetic and copies ran while one was open for 17% -> 17% of each run, Pallas kernels for 4% -> 0%
where the time goes in v2:
time: 747 us; the launch traced here: 738 us
  Pallas kernels  207 us (28%)
  waiting for transfers between devices  194 us (26%)
  matrix products  163 us (22%)
  local copies, waits for them, and re-layouts  65.5 us (9%)
  blocking collectives  39.7 us (5%)
  other arithmetic  37.4 us (5%)
  starting transfers between devices  29.2 us (4%)
    ppermute x40, waiting for transfers between devices, scatter_sum(): value = keep + lax.ppermute(send, AXES, flips)  194 us
    pallas_call x1, Pallas kernels, attend(): pl.pallas_call(functools.partial(attend_kernel, seq, scale, count), grid=...  112 us
    dot_general x4, matrix products, mm_nt(): lax.dot_general(left, right, (((1,), (1,)), ((), ())), preferred_element_...  59.6 us
    dot_general x4, matrix products, mm(): return jnp.dot(left, right, preferred_element_type=F32)  53.4 us
    pallas_call x1, Pallas kernels, attend_back(): pl.pallas_call(functools.partial(attend_back_kernel, seq, scale), grid=(i...  50 us
    dot_general x4, matrix products, mm_tn(): lax.dot_general(left, right, (((0,), (0,)), ((), ())), preferred_element_...  49.7 us
    pallas_call x1, Pallas kernels, gather(): pl.pallas_call(functools.partial(gather_kernel, count), in_specs=[anywher...  44.8 us
    unnamed x1, blocking collectives  39.7 us
  transfers between devices with their start and end apart: 40, of which 28 were waited for; matrix products, arithmetic and copies ran while one was open for 17% of the time, Pallas kernels for 0%

profile of v2, /device:TPU:0, one launch (start us, length us, event | category | flops | bytes accessed | tf_op | source)
XLA Modules:
  0.0 737.7 jit_solution(12543456836855227492)
XLA Ops:
  0.6 5.4 concatenate.32
  7.0 44.8 %gather_weights.1 = (bf16[2,2,2,4,1,384]{5,4,3,2,1,0:T(2,128)(2,1)S(1)}, bf16[2,2,2,4,32,3072]{5,4,3,2,1,0:T(8,128)(2,1)S(1)}) custom-call(bf16[1,384]{1,0:T(2,128)(2,1)S(1)} %broadcast_in_dim.4.refs_0_, bf16[32,3072]{1,0:T(8,128)(2,1)S(1)} %copy-done), custom_call_target="tpu_custom_call" | custom-call | tf_op jit(solution)/shard_map/gather_weights/pallas_call | solution.py:450
  51.8 2.7 copy-done.1
  55.5 2.4 copy.37
  63.7 11.0 %add_convert_fusion.q_ref.k_ref.v_ref = bf16[1184,3072]{1,0:T(8,128)(2,1)S(1)} fusion(bf16[1184,1024]{1,0:T(8,128)(2,1)S(1)} %bitcast.263, bf16[1024,3072]{1,0:T(8,128)(2,1)} %bitcast.230, f32[3072]{0:T(1024)S(1)} %pad_maximum_fusion.1), kind=kOutput, calls=%fused_computation.13 | convolution fusion | flops 7456358400 | bytes 16003072 | tf_op jit(solution)/shard_map/dot_general | solution.py:27
  74.8 111.8 %attend.1 = (bf16[1184,1024]{1,0:T(8,128)(2,1)S(1)}, f32[2,8,2,592]{3,2,1,0:T(2,128)S(1)}, bf16[2,2,2,4,32,1024]{5,4,3,2,1,0:T(8,128)(2,1)S(1)}, bf16[2,2,2,4,32...) custom-call(bf16[1184,3072]{1,0:T(8,128)(2,1)S(1)} %add_convert_fusion.q_ref.k_ref.v_ref, ...), custom_call_target="tpu_custom_call" | custom-call | flops 11484004352 | bytes 9699328 | tf_op jit(solution)/shard_map/attend/pallas_call | solution.py:147
  188.0 4.4 fusion.13
  192.5 2.7 reduce_sum.146
  195.2 3.1 multiply_reduce_fusion.4
  198.4 2.1 broadcast_multiply_fusion
  202.1 21.9 %multiply_convert_fusion = (bf16[1184,4096]{1,0:T(8,128)(2,1)}, f32[1184,4096]{1,0:T(8,128)}) fusion(f32[4096]{0:T(1024)S(1)} %fusion.16, bf16[1024,4096]{1,0:T(8,128)(2,1)} %bitcast.270, f32[1184,1024]{1,0:T(8,128)S(1)} %bitcast.237, f32[1024]{0:T(1024)S(1)} %reshape.297, f32[1024]{0:T(1024)S(1)} %reshape.296, f32[1184]{0:T(1024)S(1)} %add_rsqrt_fusion, ...), kind=kOutput, calls=%fused_computation.8 | convolution fusion | flops 9967271936 | bytes 42370304 | tf_op jit(solution)/shard_map/dot_general | solution.py:27
  224.0 21.4 %convert_reduce_fusion = (f32[4096]{0:T(1024)}, bf16[1184,4096]{1,0:T(8,128)(2,1)}) fusion(f32[1184,4096]{1,0:T(8,128)} %get-tuple-element.71, bf16[1184,1024]{1,0:T(8,128)(2,1)S(1)} %bitcast.254, bf16[4096,1024]{1,0:T(8,128)(2,1)S(1)} %bitcast.269), kind=kOutput, calls=%fused_computation.7 | convolution fusion | flops 10000003072 | bytes 39927808 | tf_op jit(solution)/shard_map/dot_general | solution.py:31
  245.4 19.4 %multiply_reduce_fusion = (f32[1024]{0:T(1024)}, f32[1184]{0:T(1024)S(1)}, f32[1184]{0:T(1024)S(1)}, f32[1024]{0:T(1024)}, f32[1184,1024]{1,0:T(8,128)}) fusion(f32[1184,1024]{1,0:T(8,128)S(1)} %bitcast.237, f32[1184]{0:T(1024)S(1)} %add_rsqrt_fusion, f32[1184]{0:T(1024)S(1)} %broadcast_multiply_fusion.5, f32[1024]{0:T(1024)S(1)} %reshape.296, ...), kind=kOutput, calls=%fused_computation.30 | convolution fusion | flops 9943019520 | bytes 27818496 | tf_op jit(solution)/shard_map/dot_general | solution.py:31
  264.8 4.2 convert_reduce_fusion.4
  269.1 4.1 convolution_convert_fusion.3.g_ref
  273.1 50.0 %attend_back.1 = (bf16[1184,1024]{1,0:T(8,128)(2,1)S(1)}, bf16[1184,1024]{1,0:T(8,128)(2,1)S(1)}, bf16[1184,1024]{1,0:T(8,128)(2,1)}) custom-call(bf16[1184,3072]{1,0:T(8,128)(2,1)} %copy-done.7, bf16[1184,3072]{1,0:T(8,128)(2,1)} %copy-done.7, bf16[1184,3072]{1,0:T(8,128)(2,1)} %copy-done.7, bf16[1184,1024]{1,0:T(8,128)(2,1)} %convolution_convert_fusion.3.g_ref, ...), custom_call_target="tpu_custom_call" | custom-call | flops 28710010880 | bytes 16973824 | tf_op jit(solution)/shard_map/attend_back/pallas_call | solution.py:181
  327.7 2.9 copy-done.20
  330.6 9.5 %convolution_convert_fusion.2 = bf16[1024,3072]{1,0:T(8,128)(2,1)S(1)} fusion(bf16[1184,3072]{1,0:T(8,128)(2,1)S(1)} %constant_dynamic-update-slice_fusion, f32[1184,1024]{1,0:T(8,128)S(1)} %fusion.12, f32[1024]{0:T(1024)S(1)} %copy-done.38, f32[1024]{0:T(1024)S(1)} %copy-done.35), kind=kOutput, calls=%fused_computation.16 | convolution fusion | flops 7455866880 | bytes 18423808 | tf_op jit(solution)/shard_map/dot_general | solution.py:35
  340.1 3.0 fusion.22
  343.1 2.9 dynamic-slice_bitcast_fusion.4
  346.4 2.7 dynamic-slice_bitcast_fusion.5
  349.2 5.6 convolution_convert_fusion.4
  358.2 17.8 %convolution_convert_fusion = bf16[1024,4096]{1,0:T(8,128)(2,1)} fusion(bf16[1184,4096]{1,0:T(8,128)(2,1)} %get-tuple-element.75, f32[1184,1024]{1,0:T(8,128)S(1)} %bitcast.239, f32[1024]{0:T(1024)S(1)} %reshape.297, f32[1024]{0:T(1024)S(1)} %reshape.296, f32[1184]{0:T(1024)S(1)} %add_rsqrt_fusion, f32[1184]{0:T(1024)S(1)} %broadcast_multiply_fusion.5), kind=kOutput, calls=%fused_computation.14 | convolution fusion | flops 9942368256 | bytes 22955264 | tf_op jit(solution)/shard_map/dot_general | solution.py:35
  376.0 5.3 fusion.21
  383.4 14.8 %fusion.19 = (f32[1024]{0:T(1024)S(1)}, f32[1024]{0:T(1024)S(1)}, f32[1184]{0:T(1024)S(1)}, f32[1184]{0:T(1024)S(1)}, f32[1184,1024]{1,0:T(8,128)}) fusion(f32[1184]{0:T(1024)S(1)} %copy-done.32, f32[1184]{0:T(1024)S(1)} %copy-done.31, bf16[2,577,1024]{2,1,0:T(8,128)(2,1)S(1)} %copy-done.10, f32[1184,1024]{1,0:T(8,128)} %copy-done.24, ...), kind=kOutput, calls=%fused_computation.165 | convolution fusion | flops 7461203968 | bytes 25659904 | tf_op jit(solution)/shard_map/dot_general | solution.py:31
  398.2 4.3 convert_reduce_fusion.1
  402.5 2.5 convert_reduce_fusion.3
  405.1 16.8 %convolution_convert_fusion.1 = bf16[4096,1024]{1,0:T(8,128)(2,1)} fusion(bf16[1184,4096]{1,0:T(8,128)(2,1)} %get-tuple-element.70, bf16[1184,1024]{1,0:T(8,128)(2,1)} %bitcast.255), kind=kOutput, calls=%fused_computation.15 | convolution fusion | flops 9936306176 | bytes 20512768 | tf_op jit(solution)/shard_map/dot_general | solution.py:35
  421.9 16.0 %add_convert_fusion.3 = bf16[1184,1024]{1,0:T(8,128)(2,1)S(1)} fusion(f32[1184,1024]{1,0:T(8,128)} %fusion.13, bf16[1184,4096]{1,0:T(8,128)(2,1)} %get-tuple-element.70, bf16[4096,1024]{1,0:T(8,128)(2,1)} %bitcast.266, f32[1024]{0:T(1024)S(1)} %reshape.299), kind=kOutput, calls=%fused_computation.37 | convolution fusion | flops 9935749120 | bytes 25366528 | tf_op jit(solution)/shard_map/dot_general | solution.py:27
  438.1 3.8 copy.42
  442.0 2.0 add_convert_fusion.2
  444.3 3.8 copy.43
  448.8 39.7 %all-reduce.2 = f32[32,384]{1,0:T(8,128)S(1)} all-reduce(f32[32,384]{1,0:T(8,128)S(1)} %concatenate.38), channel_id=2, replica_groups=mesh['dev'=8,'rep'=4] {'dev','rep'}, use_global_device_ids=true, to_apply=%region_16.17.clone | all-reduce | flops 12288 | bytes 98304
  488.6 5.1 fusion.20
  493.6 2.0 copy-done.18
  498.9 1.7 dynamic-slice_bitcast_fusion.3
  502.2 2.3 collective-permute-start.16
  505.7 5.7 collective-permute-done.16
  513.1 6.3 collective-permute-done.11
  520.9 3.6 collective-permute-done.17
  525.9 3.5 collective-permute-done.12
  530.6 5.7 collective-permute-done.18
  536.4 5.1 collective-permute-done.13
  541.5 3.9 collective-permute-done.19
  545.4 3.9 collective-permute-done.14
  556.3 2.0 bitcast_add_fusion.3
  562.6 10.1 %collective-permute-done.6 = bf16[2,2,2,32,1536]{4,3,2,1,0:T(8,128)(2,1)S(1)} collective-permute-done((bf16[2,2,2,32,1536]{4,3,2,1,0:T(8,128)(2,1)S(1)}, bf16[2,2,2,32,1536]{4,3,2,1,0:T(8,128)(2,1)S(1)}, u32[]{:S(2)}, u32[]{:S(2)}) %collective-permute-start.6) | collective-permute-done | bytes 786464 | tf_op jit(solution)/shard_map/ppermute | solution.py:489
  576.9 51.1 %collective-permute-done.7 = bf16[2,2,32,1536]{3,2,1,0:T(8,128)(2,1)S(1)} collective-permute-done((bf16[2,2,32,1536]{3,2,1,0:T(8,128)(2,1)S(1)}, bf16[2,2,32,1536]{3,2,1,0:T(8,128)(2,1)S(1)}, u32[]{:S(2)}, u32[]{:S(2)}) %collective-permute-start.7) | collective-permute-done | bytes 393248 | tf_op jit(solution)/shard_map/ppermute | solution.py:489
  628.9 8.9 %collective-permute-done.2 = bf16[2,2,32,1536]{3,2,1,0:T(8,128)(2,1)S(1)} collective-permute-done((bf16[2,2,32,1536]{3,2,1,0:T(8,128)(2,1)S(1)}, bf16[2,2,32,1536]{3,2,1,0:T(8,128)(2,1)S(1)}, u32[]{:S(2)}, u32[]{:S(2)}) %collective-permute-start.2) | collective-permute-done | bytes 393248 | tf_op jit(solution)/shard_map/ppermute | solution.py:489
  638.3 8.8 %collective-permute-done.8 = bf16[2,32,1536]{2,1,0:T(8,128)(2,1)S(1)} collective-permute-done((bf16[2,32,1536]{2,1,0:T(8,128)(2,1)S(1)}, bf16[2,32,1536]{2,1,0:T(8,128)(2,1)S(1)}, u32[]{:S(2)}, u32[]{:S(2)}) %collective-permute-start.8) | collective-permute-done | bytes 196640 | tf_op jit(solution)/shard_map/ppermute | solution.py:489
  647.2 10.1 %collective-permute-done.3 = bf16[2,32,1536]{2,1,0:T(8,128)(2,1)S(1)} collective-permute-done((bf16[2,32,1536]{2,1,0:T(8,128)(2,1)S(1)}, bf16[2,32,1536]{2,1,0:T(8,128)(2,1)S(1)}, u32[]{:S(2)}, u32[]{:S(2)}) %collective-permute-start.3) | collective-permute-done | bytes 196640 | tf_op jit(solution)/shard_map/ppermute | solution.py:489
  657.3 4.7 collective-permute-done.9
  662.3 4.3 collective-permute-done.4
  669.4 1.7 collective-permute-start.22
  672.4 10.1 %collective-permute-done.27 = bf16[2,2,32,2048]{3,2,1,0:T(8,128)(2,1)S(1)} collective-permute-done((bf16[2,2,32,2048]{3,2,1,0:T(8,128)(2,1)S(1)}, bf16[2,2,32,2048]{3,2,1,0:T(8,128)(2,1)S(1)}, u32[]{:S(2)}, u32[]{:S(2)}) %collective-permute-start.27) | collective-permute-done | bytes 524320 | tf_op jit(solution)/shard_map/ppermute | solution.py:489
  685.8 4.9 collective-permute-done.37
  694.0 15.5 %collective-permute-done.28 = bf16[2,32,2048]{2,1,0:T(8,128)(2,1)S(1)} collective-permute-done((bf16[2,32,2048]{2,1,0:T(8,128)(2,1)S(1)}, bf16[2,32,2048]{2,1,0:T(8,128)(2,1)S(1)}, u32[]{:S(2)}, u32[]{:S(2)}) %collective-permute-start.28) | collective-permute-done | bytes 262176 | tf_op jit(solution)/shard_map/ppermute | solution.py:489
  709.6 5.6 collective-permute-done.23
  715.3 5.5 collective-permute-done.38
  721.0 4.3 collective-permute-done.33
  725.4 2.7 collective-permute-done.29
  728.1 2.8 collective-permute-done.24
  731.8 2.0 collective-permute-done.39
  733.7 2.7 collective-permute-done.34
  (300 shorter events, 64.0 us)
Async XLA Ops:
  63.7 11.1 %copy-start.2 = (bf16[32,4096]{1,0:T(8,128)(2,1)S(1)}, bf16[32,4096]{1,0:T(8,128)(2,1)}, u32[]{:S(2)}) copy-start(bf16[32,4096]{1,0:T(8,128)(2,1)} %refs_1_.3) | copy-start | bytes 786436
  63.7 11.1 %copy-start.3 = (bf16[128,1024]{1,0:T(8,128)(2,1)S(1)}, bf16[128,1024]{1,0:T(8,128)(2,1)}, u32[]{:S(2)}) copy-start(bf16[128,1024]{1,0:T(8,128)(2,1)} %refs_2_.1) | copy-start | bytes 786436
  63.7 11.1 %copy-start.4 = (bf16[32,1024]{1,0:T(8,128)(2,1)S(1)}, bf16[32,1024]{1,0:T(8,128)(2,1)}, u32[]{:S(2)}) copy-start(bf16[32,1024]{1,0:T(8,128)(2,1)} %refs_0_.1) | copy-start | bytes 196612
  74.8 111.8 %copy-start.7 = (bf16[1184,3072]{1,0:T(8,128)(2,1)}, bf16[1184,3072]{1,0:T(8,128)(2,1)S(1)}, u32[]{:S(2)}) copy-start(bf16[1184,3072]{1,0:T(8,128)(2,1)S(1)} %add_convert_fusion.q_ref.k_ref.v_ref) | copy-start | bytes 21823492
  74.8 113.2 %copy-start.27 = (bf16[2,592,1024]{2,1,0:T(8,128)(2,1)S(1)}, bf16[2,592,1024]{2,1,0:T(8,128)(2,1)}, u32[]{:S(2)}) copy-start(bf16[2,592,1024]{2,1,0:T(8,128)(2,1)} %pad.7) | copy-start | bytes 7274500
  200.5 23.5 %copy-start.11 = (bf16[2,577,1024]{2,0,1:T(2,128)(2,1)}, bf16[2,577,1024]{2,0,1:T(2,128)(2,1)S(1)}, u32[]{:S(2)}) copy-start(bf16[2,577,1024]{2,0,1:T(2,128)(2,1)S(1)} %broadcast_multiply_fusion) | copy-start | bytes 7090180
  201.2 22.8 %slice-start.10 = ((s8[8388608]{0:T(1024)(128)(4,1)}), s8[4194304]{0:T(1024)(128)(4,1)S(1)}, s32[]{:S(2)}) async-start(s8[8388608]{0:T(1024)(128)(4,1)} %bitcast.267), calls=%async_computation.10 | async-start | bytes 8388608
  201.5 63.3 %copy-start.23 = (bf16[2,592,1024]{2,1,0:T(8,128)(2,1)}, bf16[2,592,1024]{2,1,0:T(8,128)(2,1)S(1)}, u32[]{:S(2)}) copy-start(bf16[2,592,1024]{2,1,0:T(8,128)(2,1)S(1)} %pad.8.clone) | copy-start | bytes 7274500
  202.1 21.9 %slice-start.11 = ((s8[8388608]{0:T(1024)(128)(4,1)}), s8[4194304]{0:T(1024)(128)(4,1)S(1)}, s32[]{:S(2)}) async-start(s8[8388608]{0:T(1024)(128)(4,1)} %bitcast.267), calls=%async_computation.11 | async-start | bytes 8388608
  343.1 6.1 copy-start.6
  343.1 15.1 %slice-start.4 = ((s8[4849664]{0:T(1024)(128)(4,1)}), s8[4194304]{0:T(1024)(128)(4,1)S(1)}, s32[]{:S(2)}) async-start(s8[4849664]{0:T(1024)(128)(4,1)} %bitcast.238), calls=%async_computation.4 | async-start | bytes 8388608
  345.9 204.1 %collective-permute-start.5 = (bf16[2,2,2,2,32,1536]{5,4,3,2,1,0:T(8,128)(2,1)}, bf16[2,2,2,2,32,1536]{5,4,3,2,1,0:T(8,128)(2,1)}, u32[]{:S(2)}, u32[]{:S(2)}) collective-permute-start(bf16[2,2,2,2,32,1536]{5,4,3,2,1,0:T(8,128)(2,1)} %dynamic-slice_bitcast_fusion.4), channel_id=1, source_target_pairs={{0,4},{1,5},{2,6},{3,7},{4,0},{5,1},{6,2},{7,3},{8,12},{9,13},{10,... | collective-permute-start | bytes 4718600 | tf_op jit(solution)/shard_map/ppermute | solution.py:489
  349.1 9.1 %slice-start.5 = ((s8[4849664]{0:T(1024)(128)(4,1)}), s8[655360]{0:T(1024)(128)(4,1)S(1)}, s32[]{:S(2)}) async-start(s8[4849664]{0:T(1024)(128)(4,1)} %bitcast.238), calls=%async_computation.5 | async-start | bytes 1310720
  349.1 203.1 %collective-permute-start = (bf16[2,2,2,2,32,1536]{5,4,3,2,1,0:T(8,128)(2,1)}, bf16[2,2,2,2,32,1536]{5,4,3,2,1,0:T(8,128)(2,1)}, u32[]{:S(2)}, u32[]{:S(2)}) collective-permute-start(bf16[2,2,2,2,32,1536]{5,4,3,2,1,0:T(8,128)(2,1)} %dynamic-slice_bitcast_fusion.5), channel_id=1, source_target_pairs={{0,4},{1,5},{2,6},{3,7},{4,0},{5,1},{6,2},{7,3},{8,12},{9,13},{10,... | collective-permute-start | bytes 4718600 | tf_op jit(solution)/shard_map/ppermute | solution.py:489
  354.8 28.6 %slice-start = ((s8[6291456]{0:T(1024)(128)(4,1)}), s8[4194304]{0:T(1024)(128)(4,1)S(1)}, s32[]{:S(2)}) async-start(s8[6291456]{0:T(1024)(128)(4,1)} %bitcast.231), calls=%async_computation | async-start | bytes 8388608
  356.8 144.0 %collective-permute-start.15 = (bf16[2,2,2,2,32,512]{5,4,3,2,1,0:T(8,128)(2,1)}, bf16[2,2,2,2,32,512]{5,4,3,2,1,0:T(8,128)(2,1)}, u32[]{:S(2)}, u32[]{:S(2)}) collective-permute-start(bf16[2,2,2,2,32,512]{5,4,3,2,1,0:T(8,128)(2,1)} %dynamic-slice_bitcast_fusion.16), channel_id=1, source_target_pairs={{0,4},{1,5},{2,6},{3,7},{4,0},{5,1},{6,2},{7,3},{8,12},{9,13},{10,... | collective-permute-start | bytes 1572872 | tf_op jit(solution)/shard_map/ppermute | solution.py:489
  358.0 25.4 %slice-start.1 = ((s8[6291456]{0:T(1024)(128)(4,1)}), s8[2097152]{0:T(1024)(128)(4,1)S(1)}, s32[]{:S(2)}) async-start(s8[6291456]{0:T(1024)(128)(4,1)} %bitcast.231), calls=%async_computation.1 | async-start | bytes 4194304
  358.0 144.2 %collective-permute-start.10 = (bf16[2,2,2,2,32,512]{5,4,3,2,1,0:T(8,128)(2,1)}, bf16[2,2,2,2,32,512]{5,4,3,2,1,0:T(8,128)(2,1)}, u32[]{:S(2)}, u32[]{:S(2)}) collective-permute-start(bf16[2,2,2,2,32,512]{5,4,3,2,1,0:T(8,128)(2,1)} %dynamic-slice_bitcast_fusion.17), channel_id=1, source_target_pairs={{0,4},{1,5},{2,6},{3,7},{4,0},{5,1},{6,2},{7,3},{8,12},{9,13},{10,... | collective-permute-start | bytes 1572872 | tf_op jit(solution)/shard_map/ppermute | solution.py:489
  376.0 7.4 %copy-start.10 = (bf16[2,577,1024]{2,1,0:T(8,128)(2,1)S(1)}, bf16[2,577,1024]{2,1,0:T(8,128)(2,1)}, u32[]{:S(2)}) copy-start(bf16[2,577,1024]{2,1,0:T(8,128)(2,1)} %copy-done.8) | copy-start | bytes 7090180
  381.3 16.8 %copy-start.15 = (bf16[1024,2048]{1,0:T(8,128)(2,1)}, bf16[1024,2048]{1,0:T(8,128)(2,1)S(1)}, u32[]{:S(2)}) copy-start(bf16[1024,2048]{1,0:T(8,128)(2,1)S(1)} %get-tuple-element.49) | copy-start | bytes 12582916
  382.9 172.4 %collective-permute-start.25 = (bf16[2,2,2,2,32,2048]{5,4,3,2,1,0:T(8,128)(2,1)}, bf16[2,2,2,2,32,2048]{5,4,3,2,1,0:T(8,128)(2,1)}, u32[]{:S(2)}, u32[]{:S(2)}) collective-permute-start(bf16[2,2,2,2,32,2048]{5,4,3,2,1,0:T(8,128)(2,1)} %dynamic-slice_bitcast_fusion.2), channel_id=1, source_target_pairs={{0,4},{1,5},{2,6},{3,7},{4,0},{5,1},{6,2},{7,3},{8,12},{9,13},{10,... | collective-permute-start | bytes 6291464 | tf_op jit(solution)/shard_map/ppermute | solution.py:489
  398.2 6.8 copy-start.33
  405.1 36.9 %slice-start.6 = ((s8[4849664]{0:T(1024)(128)(4,1)}), s8[4194304]{0:T(1024)(128)(4,1)S(1)}, s32[]{:S(2)}) async-start(s8[4849664]{0:T(1024)(128)(4,1)} %bitcast.240), calls=%async_computation.6 | async-start | bytes 8388608
  405.1 36.9 %slice-start.8 = ((s8[4849664]{0:T(1024)(128)(4,1)}), s8[4194304]{0:T(1024)(128)(4,1)S(1)}, s32[]{:S(2)}) async-start(s8[4849664]{0:T(1024)(128)(4,1)} %bitcast.257), calls=%async_computation.8 | async-start | bytes 8388608
  421.9 20.1 %slice-start.7 = ((s8[4849664]{0:T(1024)(128)(4,1)}), s8[655360]{0:T(1024)(128)(4,1)S(1)}, s32[]{:S(2)}) async-start(s8[4849664]{0:T(1024)(128)(4,1)} %bitcast.240), calls=%async_computation.7 | async-start | bytes 1310720
  421.9 20.1 %slice-start.9 = ((s8[4849664]{0:T(1024)(128)(4,1)}), s8[655360]{0:T(1024)(128)(4,1)S(1)}, s32[]{:S(2)}) async-start(s8[4849664]{0:T(1024)(128)(4,1)} %bitcast.257), calls=%async_computation.9 | async-start | bytes 1310720
  500.8 48.5 %copy-start.30 = (bf16[2,2,2,2,128,512]{5,4,3,2,1,0:T(8,128)(2,1)S(1)}, bf16[2,2,2,2,128,512]{5,4,3,2,1,0:T(8,128)(2,1)}, u32[]{:S(2)}) copy-start(bf16[2,2,2,2,128,512]{5,4,3,2,1,0:T(8,128)(2,1)} %dynamic-slice_bitcast_fusion) | copy-start | bytes 6291460
  500.8 49.7 %copy-start.22 = (bf16[1024,1536]{1,0:T(8,128)(2,1)S(1)}, bf16[1024,1536]{1,0:T(8,128)(2,1)}, u32[]{:S(2)}) copy-start(bf16[1024,1536]{1,0:T(8,128)(2,1)} %get-tuple-element.51) | copy-start | bytes 9437188
  500.9 57.6 %collective-permute-start.20 = (bf16[2,2,2,2,32,2048]{5,4,3,2,1,0:T(8,128)(2,1)S(1)}, bf16[2,2,2,2,32,2048]{5,4,3,2,1,0:T(8,128)(2,1)S(1)}, u32[]{:S(2)}, u32[]{:S(2)}) collective-permute-start(bf16[2,2,2,2,32,2048]{5,4,3,2,1,0:T(8,128)(2,1)S(1)} %dynamic-slice_bitcast_fusion.3), channel_id=1, source_target_pairs={{0,4},{1,5},{2,6},{3,7},{4,0},{5,1},{6,2},{7,3},{8,12},{9,13},{10,... | collective-permute-start | bytes 6291464 | tf_op jit(solution)/shard_map/ppermute | solution.py:489
  502.2 9.1 %collective-permute-start.16 = (bf16[2,2,2,32,512]{4,3,2,1,0:T(8,128)(2,1)S(1)}, bf16[2,2,2,32,512]{4,3,2,1,0:T(8,128)(2,1)S(1)}, u32[]{:S(2)}, u32[]{:S(2)}) collective-permute-start(bf16[2,2,2,32,512]{4,3,2,1,0:T(8,128)(2,1)S(1)} %dynamic-slice_bitcast_fusion.24), channel_id=1, source_target_pairs={{0,16},{1,17},{2,18},{3,19},{4,20},{5,21},{6,22},{7,23},{8,24},{9,... | collective-permute-start | bytes 786440 | tf_op jit(solution)/shard_map/ppermute | solution.py:489
  511.4 8.1 %collective-permute-start.11 = (bf16[2,2,2,32,512]{4,3,2,1,0:T(8,128)(2,1)S(1)}, bf16[2,2,2,32,512]{4,3,2,1,0:T(8,128)(2,1)S(1)}, u32[]{:S(2)}, u32[]{:S(2)}) collective-permute-start(bf16[2,2,2,32,512]{4,3,2,1,0:T(8,128)(2,1)S(1)} %dynamic-slice_bitcast_fusion.25), channel_id=1, source_target_pairs={{0,8},{1,9},{2,10},{3,11},{4,12},{5,13},{6,14},{7,15},{8,0},{9,1},... | collective-permute-start | bytes 786440 | tf_op jit(solution)/shard_map/ppermute | solution.py:489
  513.1 40.6 %copy-start.21 = (bf16[1024,1536]{1,0:T(8,128)(2,1)S(1)}, bf16[1024,1536]{1,0:T(8,128)(2,1)}, u32[]{:S(2)}) copy-start(bf16[1024,1536]{1,0:T(8,128)(2,1)} %get-tuple-element.50) | copy-start | bytes 9437188
  519.5 5.0 collective-permute-start.17
  524.4 5.0 collective-permute-start.12
  529.4 6.9 collective-permute-start.18
  536.3 5.2 collective-permute-start.13
  541.5 3.9 collective-permute-start.19
  545.4 3.9 collective-permute-start.14
  549.3 10.7 %collective-permute-start.35 = (bf16[2,2,2,2,128,512]{5,4,3,2,1,0:T(8,128)(2,1)S(1)}, bf16[2,2,2,2,128,512]{5,4,3,2,1,0:T(8,128)(2,1)S(1)}, u32[]{:S(2)}, u32[]{:S(2)}) collective-permute-start(bf16[2,2,2,2,128,512]{5,4,3,2,1,0:T(8,128)(2,1)S(1)} %copy-done.30), channel_id=1, source_target_pairs={{0,4},{1,5},{2,6},{3,7},{4,0},{5,1},{6,2},{7,3},{8,12},{9,13},{10,... | collective-permute-start | bytes 6291464 | tf_op jit(solution)/shard_map/ppermute | solution.py:489
  550.0 11.5 %collective-permute-start.30 = (bf16[2,2,2,2,128,512]{5,4,3,2,1,0:T(8,128)(2,1)S(1)}, bf16[2,2,2,2,128,512]{5,4,3,2,1,0:T(8,128)(2,1)S(1)}, u32[]{:S(2)}, u32[]{:S(2)}) collective-permute-start(bf16[2,2,2,2,128,512]{5,4,3,2,1,0:T(8,128)(2,1)S(1)} %dynamic-slice_bitcast_fusion.1), channel_id=1, source_target_pairs={{0,4},{1,5},{2,6},{3,7},{4,0},{5,1},{6,2},{7,3},{8,12},{9,13},{10,... | collective-permute-start | bytes 6291464 | tf_op jit(solution)/shard_map/ppermute | solution.py:489
  552.2 20.5 %collective-permute-start.6 = (bf16[2,2,2,32,1536]{4,3,2,1,0:T(8,128)(2,1)S(1)}, bf16[2,2,2,32,1536]{4,3,2,1,0:T(8,128)(2,1)S(1)}, u32[]{:S(2)}, u32[]{:S(2)}) collective-permute-start(bf16[2,2,2,32,1536]{4,3,2,1,0:T(8,128)(2,1)S(1)} %dynamic-slice_bitcast_fusion.10), channel_id=1, source_target_pairs={{0,16},{1,17},{2,18},{3,19},{4,20},{5,21},{6,22},{7,23},{8,24},{9,... | collective-permute-start | bytes 2359304 | tf_op jit(solution)/shard_map/ppermute | solution.py:489
  555.4 20.5 %collective-permute-start.1 = (bf16[2,2,2,32,1536]{4,3,2,1,0:T(8,128)(2,1)S(1)}, bf16[2,2,2,32,1536]{4,3,2,1,0:T(8,128)(2,1)S(1)}, u32[]{:S(2)}, u32[]{:S(2)}) collective-permute-start(bf16[2,2,2,32,1536]{4,3,2,1,0:T(8,128)(2,1)S(1)} %dynamic-slice_bitcast_fusion.11), channel_id=1, source_target_pairs={{0,8},{1,9},{2,10},{3,11},{4,12},{5,13},{6,14},{7,15},{8,0},{9,1},... | collective-permute-start | bytes 2359304 | tf_op jit(solution)/shard_map/ppermute | solution.py:489
  558.5 108.9 %collective-permute-start.26 = (bf16[2,2,2,32,2048]{4,3,2,1,0:T(8,128)(2,1)S(1)}, bf16[2,2,2,32,2048]{4,3,2,1,0:T(8,128)(2,1)S(1)}, u32[]{:S(2)}, u32[]{:S(2)}) collective-permute-start(bf16[2,2,2,32,2048]{4,3,2,1,0:T(8,128)(2,1)S(1)} %dynamic-slice_bitcast_fusion.8), channel_id=1, source_target_pairs={{0,16},{1,17},{2,18},{3,19},{4,20},{5,21},{6,22},{7,23},{8,24},{9,... | collective-permute-start | bytes 3145736 | tf_op jit(solution)/shard_map/ppermute | solution.py:489
  560.0 109.3 %collective-permute-start.21 = (bf16[2,2,2,32,2048]{4,3,2,1,0:T(8,128)(2,1)S(1)}, bf16[2,2,2,32,2048]{4,3,2,1,0:T(8,128)(2,1)S(1)}, u32[]{:S(2)}, u32[]{:S(2)}) collective-permute-start(bf16[2,2,2,32,2048]{4,3,2,1,0:T(8,128)(2,1)S(1)} %dynamic-slice_bitcast_fusion.9), channel_id=1, source_target_pairs={{0,8},{1,9},{2,10},{3,11},{4,12},{5,13},{6,14},{7,15},{8,0},{9,1},... | collective-permute-start | bytes 3145736 | tf_op jit(solution)/shard_map/ppermute | solution.py:489
  561.5 109.7 %collective-permute-start.36 = (bf16[2,2,2,128,512]{4,3,2,1,0:T(8,128)(2,1)S(1)}, bf16[2,2,2,128,512]{4,3,2,1,0:T(8,128)(2,1)S(1)}, u32[]{:S(2)}, u32[]{:S(2)}) collective-permute-start(bf16[2,2,2,128,512]{4,3,2,1,0:T(8,128)(2,1)S(1)} %dynamic-slice_bitcast_fusion.6), channel_id=1, source_target_pairs={{0,16},{1,17},{2,18},{3,19},{4,20},{5,21},{6,22},{7,23},{8,24},{9,... | collective-permute-start | bytes 3145736 | tf_op jit(solution)/shard_map/ppermute | solution.py:489
  572.7 98.7 %collective-permute-start.31 = (bf16[2,2,2,128,512]{4,3,2,1,0:T(8,128)(2,1)S(1)}, bf16[2,2,2,128,512]{4,3,2,1,0:T(8,128)(2,1)S(1)}, u32[]{:S(2)}, u32[]{:S(2)}) collective-permute-start(bf16[2,2,2,128,512]{4,3,2,1,0:T(8,128)(2,1)S(1)} %dynamic-slice_bitcast_fusion.7), channel_id=1, source_target_pairs={{0,8},{1,9},{2,10},{3,11},{4,12},{5,13},{6,14},{7,15},{8,0},{9,1},... | collective-permute-start | bytes 3145736 | tf_op jit(solution)/shard_map/ppermute | solution.py:489
  575.9 52.1 %collective-permute-start.7 = (bf16[2,2,32,1536]{3,2,1,0:T(8,128)(2,1)S(1)}, bf16[2,2,32,1536]{3,2,1,0:T(8,128)(2,1)S(1)}, u32[]{:S(2)}, u32[]{:S(2)}) collective-permute-start(bf16[2,2,32,1536]{3,2,1,0:T(8,128)(2,1)S(1)} %dynamic-slice_bitcast_fusion.18), channel_id=1, source_target_pairs={{0,8},{1,9},{2,10},{3,11},{4,12},{5,13},{6,14},{7,15},{8,0},{9,1},... | collective-permute-start | bytes 1179656 | tf_op jit(solution)/shard_map/ppermute | solution.py:489
  628.0 9.9 %collective-permute-start.2 = (bf16[2,2,32,1536]{3,2,1,0:T(8,128)(2,1)S(1)}, bf16[2,2,32,1536]{3,2,1,0:T(8,128)(2,1)S(1)}, u32[]{:S(2)}, u32[]{:S(2)}) collective-permute-start(bf16[2,2,32,1536]{3,2,1,0:T(8,128)(2,1)S(1)} %dynamic-slice_bitcast_fusion.19), channel_id=1, source_target_pairs={{0,16},{1,17},{2,18},{3,19},{4,20},{5,21},{6,22},{7,23},{8,24},{9,... | collective-permute-start | bytes 1179656 | tf_op jit(solution)/shard_map/ppermute | solution.py:489
  637.9 9.3 %collective-permute-start.8 = (bf16[2,32,1536]{2,1,0:T(8,128)(2,1)S(1)}, bf16[2,32,1536]{2,1,0:T(8,128)(2,1)S(1)}, u32[]{:S(2)}, u32[]{:S(2)}) collective-permute-start(bf16[2,32,1536]{2,1,0:T(8,128)(2,1)S(1)} %dynamic-slice_bitcast_fusion.26), channel_id=1, source_target_pairs={{0,2},{1,3},{2,0},{3,1},{4,6},{5,7},{6,4},{7,5},{8,10},{9,11},{10,... | collective-permute-start | bytes 589832 | tf_op jit(solution)/shard_map/ppermute | solution.py:489
  647.1 10.1 %collective-permute-start.3 = (bf16[2,32,1536]{2,1,0:T(8,128)(2,1)S(1)}, bf16[2,32,1536]{2,1,0:T(8,128)(2,1)S(1)}, u32[]{:S(2)}, u32[]{:S(2)}) collective-permute-start(bf16[2,32,1536]{2,1,0:T(8,128)(2,1)S(1)} %dynamic-slice_bitcast_fusion.27), channel_id=1, source_target_pairs={{0,2},{1,3},{2,0},{3,1},{4,6},{5,7},{6,4},{7,5},{8,10},{9,11},{10,... | collective-permute-start | bytes 589832 | tf_op jit(solution)/shard_map/ppermute | solution.py:489
  657.3 4.7 collective-permute-start.9
  662.0 4.6 collective-permute-start.4
  667.6 14.9 %collective-permute-start.27 = (bf16[2,2,32,2048]{3,2,1,0:T(8,128)(2,1)S(1)}, bf16[2,2,32,2048]{3,2,1,0:T(8,128)(2,1)S(1)}, u32[]{:S(2)}, u32[]{:S(2)}) collective-permute-start(bf16[2,2,32,2048]{3,2,1,0:T(8,128)(2,1)S(1)} %dynamic-slice_bitcast_fusion.14), channel_id=1, source_target_pairs={{0,8},{1,9},{2,10},{3,11},{4,12},{5,13},{6,14},{7,15},{8,0},{9,1},... | collective-permute-start | bytes 1572872 | tf_op jit(solution)/shard_map/ppermute | solution.py:489
  669.4 14.9 %collective-permute-start.22 = (bf16[2,2,32,2048]{3,2,1,0:T(8,128)(2,1)S(1)}, bf16[2,2,32,2048]{3,2,1,0:T(8,128)(2,1)S(1)}, u32[]{:S(2)}, u32[]{:S(2)}) collective-permute-start(bf16[2,2,32,2048]{3,2,1,0:T(8,128)(2,1)S(1)} %dynamic-slice_bitcast_fusion.15), channel_id=1, source_target_pairs={{0,16},{1,17},{2,18},{3,19},{4,20},{5,21},{6,22},{7,23},{8,24},{9,... | collective-permute-start | bytes 1572872 | tf_op jit(solution)/shard_map/ppermute | solution.py:489
  671.3 19.4 %collective-permute-start.37 = (bf16[2,2,128,512]{3,2,1,0:T(8,128)(2,1)S(1)}, bf16[2,2,128,512]{3,2,1,0:T(8,128)(2,1)S(1)}, u32[]{:S(2)}, u32[]{:S(2)}) collective-permute-start(bf16[2,2,128,512]{3,2,1,0:T(8,128)(2,1)S(1)} %dynamic-slice_bitcast_fusion.12), channel_id=1, source_target_pairs={{0,8},{1,9},{2,10},{3,11},{4,12},{5,13},{6,14},{7,15},{8,0},{9,1},... | collective-permute-start | bytes 1572872 | tf_op jit(solution)/shard_map/ppermute | solution.py:489
  671.6 20.6 %collective-permute-start.32 = (bf16[2,2,128,512]{3,2,1,0:T(8,128)(2,1)S(1)}, bf16[2,2,128,512]{3,2,1,0:T(8,128)(2,1)S(1)}, u32[]{:S(2)}, u32[]{:S(2)}) collective-permute-start(bf16[2,2,128,512]{3,2,1,0:T(8,128)(2,1)S(1)} %dynamic-slice_bitcast_fusion.13), channel_id=1, source_target_pairs={{0,16},{1,17},{2,18},{3,19},{4,20},{5,21},{6,22},{7,23},{8,24},{9,... | collective-permute-start | bytes 1572872 | tf_op jit(solution)/shard_map/ppermute | solution.py:489
  682.6 26.9 %collective-permute-start.28 = (bf16[2,32,2048]{2,1,0:T(8,128)(2,1)S(1)}, bf16[2,32,2048]{2,1,0:T(8,128)(2,1)S(1)}, u32[]{:S(2)}, u32[]{:S(2)}) collective-permute-start(bf16[2,32,2048]{2,1,0:T(8,128)(2,1)S(1)} %dynamic-slice_bitcast_fusion.22), channel_id=1, source_target_pairs={{0,2},{1,3},{2,0},{3,1},{4,6},{5,7},{6,4},{7,5},{8,10},{9,11},{10,... | collective-permute-start | bytes 786440 | tf_op jit(solution)/shard_map/ppermute | solution.py:489
  684.5 30.7 %collective-permute-start.23 = (bf16[2,32,2048]{2,1,0:T(8,128)(2,1)S(1)}, bf16[2,32,2048]{2,1,0:T(8,128)(2,1)S(1)}, u32[]{:S(2)}, u32[]{:S(2)}) collective-permute-start(bf16[2,32,2048]{2,1,0:T(8,128)(2,1)S(1)} %dynamic-slice_bitcast_fusion.23), channel_id=1, source_target_pairs={{0,2},{1,3},{2,0},{3,1},{4,6},{5,7},{6,4},{7,5},{8,10},{9,11},{10,... | collective-permute-start | bytes 786440 | tf_op jit(solution)/shard_map/ppermute | solution.py:489
  690.8 30.0 %collective-permute-start.38 = (bf16[2,128,512]{2,1,0:T(8,128)(2,1)S(1)}, bf16[2,128,512]{2,1,0:T(8,128)(2,1)S(1)}, u32[]{:S(2)}, u32[]{:S(2)}) collective-permute-start(bf16[2,128,512]{2,1,0:T(8,128)(2,1)S(1)} %dynamic-slice_bitcast_fusion.20), channel_id=1, source_target_pairs={{0,2},{1,3},{2,0},{3,1},{4,6},{5,7},{6,4},{7,5},{8,10},{9,11},{10,... | collective-permute-start | bytes 786440 | tf_op jit(solution)/shard_map/ppermute | solution.py:489
  692.3 33.0 %collective-permute-start.33 = (bf16[2,128,512]{2,1,0:T(8,128)(2,1)S(1)}, bf16[2,128,512]{2,1,0:T(8,128)(2,1)S(1)}, u32[]{:S(2)}, u32[]{:S(2)}) collective-permute-start(bf16[2,128,512]{2,1,0:T(8,128)(2,1)S(1)} %dynamic-slice_bitcast_fusion.21), channel_id=1, source_target_pairs={{0,2},{1,3},{2,0},{3,1},{4,6},{5,7},{6,4},{7,5},{8,10},{9,11},{10,... | collective-permute-start | bytes 786440 | tf_op jit(solution)/shard_map/ppermute | solution.py:489
  709.5 18.5 %collective-permute-start.29 = (bf16[32,2048]{1,0:T(8,128)(2,1)S(1)}, bf16[32,2048]{1,0:T(8,128)(2,1)S(1)}, u32[]{:S(2)}, u32[]{:S(2)}) collective-permute-start(bf16[32,2048]{1,0:T(8,128)(2,1)S(1)} %dynamic-slice_bitcast_fusion.30), channel_id=1, source_target_pairs={{0,1},{1,0},{2,3},{3,2},{4,5},{5,4},{6,7},{7,6},{8,9},{9,8},{10,11... | collective-permute-start | bytes 393224 | tf_op jit(solution)/shard_map/ppermute | solution.py:489
  715.3 15.6 %collective-permute-start.24 = (bf16[32,2048]{1,0:T(8,128)(2,1)S(1)}, bf16[32,2048]{1,0:T(8,128)(2,1)S(1)}, u32[]{:S(2)}, u32[]{:S(2)}) collective-permute-start(bf16[32,2048]{1,0:T(8,128)(2,1)S(1)} %dynamic-slice_bitcast_fusion.31), channel_id=1, source_target_pairs={{0,1},{1,0},{2,3},{3,2},{4,5},{5,4},{6,7},{7,6},{8,9},{9,8},{10,11... | collective-permute-start | bytes 393224 | tf_op jit(solution)/shard_map/ppermute | solution.py:489
  720.9 12.8 %collective-permute-start.39 = (bf16[128,512]{1,0:T(8,128)(2,1)S(1)}, bf16[128,512]{1,0:T(8,128)(2,1)S(1)}, u32[]{:S(2)}, u32[]{:S(2)}) collective-permute-start(bf16[128,512]{1,0:T(8,128)(2,1)S(1)} %dynamic-slice_bitcast_fusion.28), channel_id=1, source_target_pairs={{0,1},{1,0},{2,3},{3,2},{4,5},{5,4},{6,7},{7,6},{8,9},{9,8},{10,11... | collective-permute-start | bytes 393224 | tf_op jit(solution)/shard_map/ppermute | solution.py:489
  725.4 11.1 %collective-permute-start.34 = (bf16[128,512]{1,0:T(8,128)(2,1)S(1)}, bf16[128,512]{1,0:T(8,128)(2,1)S(1)}, u32[]{:S(2)}, u32[]{:S(2)}) collective-permute-start(bf16[128,512]{1,0:T(8,128)(2,1)S(1)} %dynamic-slice_bitcast_fusion.29), channel_id=1, source_target_pairs={{0,1},{1,0},{2,3},{3,2},{4,5},{5,4},{6,7},{7,6},{8,9},{9,8},{10,11... | collective-permute-start | bytes 393224 | tf_op jit(solution)/shard_map/ppermute | solution.py:489
  (31 other events, 103.5 us)
